TPU v7x, 512 devices: a whole 4x8x8 slice. The times are simulated.
512 devices in a mesh: shards: 16 (over z, core), tensor: 4 (over x), sections: 8 (over y).
Axes of the slice: x: 4, y: 8, z: 8, core: 2. Of those that a mesh axis runs over, the one named last changes fastest.
Arguments:
- replica_grads: bfloat16 [16, 8, 2, 1536, 512], P('shards', 'sections', None, None, 'tensor'), may hold values from -6 to 6
- error_feedback: bfloat16 [16, 8, 2, 1536, 512], P('shards', 'sections', None, None, 'tensor'), may hold values from -3 to 3
- q_start: float32 [8, 2, 512, 32], P('sections', None, 'tensor'), may hold values from -0.25 to 0.25
- gram_root: float32 [8, 2, 32, 32], P('sections'), may hold values from -2 to 2
- momentum: float32 [8, 2, 1536, 512], P('sections', None, 'shards', 'tensor'), may hold values from -1.2 to 1.2
- weights: float32 [8, 2, 1536, 512], P('sections', None, 'shards', 'tensor'), may hold values from -3 to 3
- router_partials: bfloat16 [512, 1536, 40], P(('shards', 'tensor', 'sections')), may hold values from -12 to 12
- gain_partials: bfloat16 [512, 2, 1536], P(('shards', 'tensor', 'sections')), may hold values from -12 to 12
- router_momentum: float32 [1536, 40], P('shards'), may hold values from -1.2 to 1.2
- router_weights: float32 [1536, 40], P('shards'), may hold values from -3 to 3
- gain_momentum: float32 [2, 1536], P(None, 'shards'), may hold values from -1.2 to 1.2
- gain_weights: float32 [2, 1536], P(None, 'shards'), may hold values from 0.1 to 1.9
Outputs:
- new_error: bfloat16 [16, 8, 2, 1536, 512], P('shards', 'sections', None, None, 'tensor')
- new_momentum: float32 [8, 2, 1536, 512], P('sections', None, 'shards', 'tensor')
- new_weights: float32 [8, 2, 1536, 512], P('sections', None, None, 'tensor')
- new_router_momentum: float32 [1536, 40], P('shards')
- new_router_weights: float32 [1536, 40], replicated
- new_gain_momentum: float32 [2, 1536], P(None, 'shards')
- new_gain_weights: float32 [2, 1536], replicated
All inputs are finite; a program needn't handle non-finite values.
Results may differ from a plain program's by a relative error of at most 0.001.
Values sent between devices are 32-bit elements; how exact they have to be, the bound alone decides.
No kernel may reach another device: no remote copies, remote signals or barrier semaphores. Data moves between devices by JAX's collectives and lax.ppermute only.
A program may use at most 64 MiB of HBM per device.

v0:
```python
import jax
import jax.numpy as jnp
from jax import lax
from jax.sharding import PartitionSpec as P

momentum_decay = 0.9
step_size = 0.5


def per_device(
    replica_grads,
    error_feedback,
    q_start,
    gram_root,
    momentum,
    weights,
    router_partials,
    gain_partials,
    router_momentum,
    router_weights,
    gain_momentum,
    gain_weights,
):
    shard_count = lax.axis_size("shards")
    shard_index = lax.axis_index("shards")
    rows = momentum.shape[2]
    start = shard_index * rows
    highest = lax.Precision.HIGHEST
    combined = replica_grads[0].astype(jnp.float32) + error_feedback[0].astype(jnp.float32)
    p_local = jnp.einsum("ekdf,ekfr->ekdr", combined, q_start, precision=highest)
    router_term = router_partials[0].astype(jnp.float32)
    gain_term = gain_partials[0].astype(jnp.float32)
    p_total = lax.psum(p_local, ("shards", "tensor"))
    router_total, gain_total = lax.psum((router_term, gain_term), ("shards", "tensor", "sections"))
    router_rows = lax.dynamic_slice_in_dim(router_total / shard_count, start, rows, 0)
    gain_rows = lax.dynamic_slice_in_dim(gain_total / shard_count, start, rows, 1)
    p_avg = p_total / shard_count
    p_hat = jnp.einsum("ekdr,ekrt->ekdt", p_avg, gram_root, precision=highest)
    q_local = jnp.einsum("ekdf,ekdr->ekfr", combined, p_hat, precision=highest)
    q_avg = lax.psum(q_local, "shards") / shard_count
    approx = jnp.einsum("ekdr,ekfr->ekdf", p_hat, q_avg, precision=highest)
    new_error = (combined - approx).astype(jnp.bfloat16)[None]
    new_router_momentum = momentum_decay * router_momentum + router_rows
    router_part = router_weights - step_size * new_router_momentum
    new_gain_momentum = momentum_decay * gain_momentum + gain_rows
    gain_part = gain_weights - step_size * new_gain_momentum
    approx_rows = lax.dynamic_slice_in_dim(approx, start, rows, 2)
    new_momentum = momentum_decay * momentum + approx_rows
    weight_rows = weights - step_size * new_momentum
    new_weights, new_router_weights, new_gain_weights = (
        lax.all_gather(weight_rows, "shards", axis=2, tiled=True),
        lax.all_gather(router_part, "shards", axis=0, tiled=True),
        lax.all_gather(gain_part, "shards", axis=1, tiled=True),
    )
    return (
        new_error,
        new_momentum,
        new_weights,
        new_router_momentum,
        new_router_weights,
        new_gain_momentum,
        new_gain_weights,
    )


def solution(mesh):
    return jax.shard_map(
        per_device,
        mesh=mesh,
        in_specs=(
            P("shards", "sections", None, None, "tensor"),
            P("shards", "sections", None, None, "tensor"),
            P("sections", None, "tensor", None),
            P("sections", None, None, None),
            P("sections", None, "shards", "tensor"),
            P("sections", None, "shards", "tensor"),
            P(("shards", "tensor", "sections"), None, None),
            P(("shards", "tensor", "sections"), None, None),
            P("shards", None),
            P("shards", None),
            P(None, "shards"),
            P(None, "shards"),
        ),
        out_specs=(
            P("shards", "sections", None, None, "tensor"),
            P("sections", None, "shards", "tensor"),
            P("sections", None, None, "tensor"),
            P("shards", None),
            P(),
            P(None, "shards"),
            P(),
        ),
        check_vma=False,
    )
```

profile of v0, /device:TPU:1, one launch (start us, length us, event | category | flops | bytes accessed | tf_op | source)
XLA Modules:
  0.0 531.9 jit_solution(9592228355170978360)
XLA Ops:
  7.2 0.0 copy-start
  7.2 0.0 copy-start.1
  7.2 0.0 copy-start.2
  7.2 0.0 copy-start.4
  7.2 0.0 copy-start.7
  7.2 0.0 all-reduce.3.cloned.1.call-start
  7.3 0.7 copy-done
  7.9 3.9 convolution_bitcast_fusion
  11.9 0.0 all-reduce.3.cloned.1.call-update
  11.9 0.0 all-reduce.5.cloned.1.call-start
  11.9 0.0 copy-done.4
  11.9 0.7 bitcast_convert_fusion
  12.6 0.0 all-reduce.5.cloned.1.call-update
  12.7 0.0 all-gather.4.cloned.1.call-start
  12.7 195.2 %all-reduce.3.cloned.1.call-done = f32[1,2,1536,32]{2,3,1,0:T(8,128)} async-done(((f32[1,2,1536,32]{2,3,1,0:T(8,128)}), f32[1,2,1536,32]{2,3,1,0:T(8,128)}) %all-reduce.3.cloned.1.call-update) | async-done | bytes 393232 | tf_op jit(solution)/shard_map/psum | solution.py:33
  207.9 0.0 copy-done.7
  207.9 1.5 fusion.8
  209.4 0.0 copy-start.3
  209.4 0.7 copy-done.3
  210.2 0.0 copy-done.1
  210.2 0.0 copy-done.2
  210.2 1.1 fusion.4
  211.3 0.0 copy-start.10
  211.3 0.0 copy-start.11
  211.3 0.0 copy-start.12
  211.4 0.0 copy-start.8
  211.4 0.0 copy-start.9
  211.4 46.7 %psum.29 = f32[1,2,128,32]{2,3,1,0:T(8,128)S(1)} all-reduce(f32[1,2,128,32]{2,3,1,0:T(8,128)S(1)} %fusion.4), channel_id=1, replica_groups=mesh['shards'=16,'tensor'=4,'sections'=8] {'shards'}, use_global_device_ids=true, to_apply=%region_1.0 | all-reduce | flops 8192 | bytes 65536 | tf_op jit(solution)/shard_map/psum | solution.py:40
  258.0 3.6 fusion.12
  261.7 0.0 copy-done.5
  261.7 0.0 copy-done.6
  261.7 0.7 multiply_subtract_fusion
  262.4 0.0 all-gather.4.cloned.1.call-update
  262.4 0.0 copy-done.10
  262.4 99.3 %psum.31 = f32[2,1536]{1,0:T(2,128)S(1)} all-reduce(f32[2,1536]{1,0:T(2,128)S(1)} %bitcast_convert_fusion.1), channel_id=1, replica_groups=mesh['shards'=16,'tensor'=4,'sections'=8] {'shards','tensor','sections'}, use_global_device_ids=true, to_apply=%region_3.0 | all-reduce | flops 3072 | bytes 24576 | tf_op jit(solution)/shard_map/psum | solution.py:34
  361.8 0.0 copy-done.11
  361.8 0.6 subtract_bitcast_fusion.1
  362.4 16.6 %all-gather.1 = f32[16,96,2]{1,2,0:T(2,128)S(1)} all-gather(f32[1,96,2]{1,2,0:T(2,128)S(1)} %get-tuple-element.7), channel_id=1, replica_groups=mesh['shards'=16,'tensor'=4,'sections'=8] {'shards'}, dimensions={0}, use_global_device_ids=true | all-gather | bytes 13056 | tf_op jit(solution)/shard_map/all_gather | solution.py:53
  379.0 0.7 reshape.67
  379.7 101.5 %all-reduce.5.cloned.1.call-done = f32[1536,40]{0,1:T(8,128)} async-done(((f32[1536,40]{0,1:T(8,128)}), f32[1536,40]{0,1:T(8,128)}) %all-reduce.5.cloned.1.call-update) | async-done | bytes 245776 | tf_op jit(solution)/shard_map/psum | solution.py:34
  481.2 0.0 copy-done.8
  481.2 1.5 subtract_bitcast_fusion
  482.6 17.2 %all-gather = f32[16,96,40]{1,2,0:T(8,128)S(1)} all-gather(f32[1,96,40]{1,2,0:T(8,128)S(1)} %get-tuple-element.9), channel_id=1, replica_groups=mesh['shards'=16,'tensor'=4,'sections'=8] {'shards'}, dimensions={0}, use_global_device_ids=true | all-gather | bytes 261120 | tf_op jit(solution)/shard_map/all_gather | solution.py:52
  499.9 0.1 copy.24
  499.9 0.9 reshape.65
  500.8 1.1 fusion.7
  501.9 20.8 %all-gather.4.cloned.1.call-done = f32[1,2,1536,128]{3,2,1,0:T(8,128)} async-done(((f32[1,2,96,128]{3,2,1,0:T(8,128)}), f32[1,2,1536,128]{3,2,1,0:T(8,128)}) %all-gather.4.cloned.1.call-update) | async-done | bytes 1572880 | tf_op jit(solution)/shard_map/all_gather | solution.py:51
  522.7 2.7 copy.30
  (6 shorter events, 0.0 us)
Async XLA Ops:
  7.2 0.8 copy-start
  7.2 203.0 %copy-start.1 = (bf16[1,1,2,1536,128]{4,3,2,1,0:T(8,128)(2,1)S(1)}, bf16[1,1,2,1536,128]{4,3,2,1,0:T(8,128)(2,1)}, u32[]{:S(2)}) copy-start(bf16[1,1,2,1536,128]{4,3,2,1,0:T(8,128)(2,1)} %param.13) | copy-start | bytes 2359300
  7.2 203.0 %copy-start.2 = (bf16[1,1,2,1536,128]{4,3,2,1,0:T(8,128)(2,1)S(1)}, bf16[1,1,2,1536,128]{4,3,2,1,0:T(8,128)(2,1)}, u32[]{:S(2)}) copy-start(bf16[1,1,2,1536,128]{4,3,2,1,0:T(8,128)(2,1)} %param.12) | copy-start | bytes 2359300
  7.2 4.7 copy-start.4
  7.2 200.7 %copy-start.7 = (f32[1,2,32,32]{3,2,1,0:T(8,128)S(1)}, f32[1,2,32,32]{3,2,1,0:T(8,128)}, u32[]{:S(2)}) copy-start(f32[1,2,32,32]{3,2,1,0:T(8,128)} %param.15) | copy-start | bytes 24580
  7.2 200.7 %all-reduce.3.cloned.1.call-start = ((), (), s32[]{:S(2)}) async-start(), calls=%async_computation | async-start | bytes 786432 | tf_op jit(solution)/shard_map/psum | solution.py:33
  11.9 469.3 %all-reduce.5.cloned.1.call-start = ((), (), s32[]{:S(2)}) async-start(), calls=%async_computation.2 | async-start | bytes 491520 | tf_op jit(solution)/shard_map/psum | solution.py:34
  12.7 510.0 %all-gather.4.cloned.1.call-start = ((), (), s32[]{:S(2)}) async-start(), calls=%async_computation.1 | async-start | bytes 1671168 | tf_op jit(solution)/shard_map/all_gather | solution.py:51
  209.4 0.7 copy-start.3
  210.2 51.5 %copy-start.5 = (f32[1,2,96,128]{3,2,1,0:T(8,128)S(1)}, f32[1,2,96,128]{3,2,1,0:T(8,128)}, u32[]{:S(2)}) copy-start(f32[1,2,96,128]{3,2,1,0:T(8,128)} %param.17) | copy-start | bytes 294916
  210.2 51.5 %copy-start.6 = (f32[1,2,96,128]{3,2,1,0:T(8,128)S(1)}, f32[1,2,96,128]{3,2,1,0:T(8,128)}, u32[]{:S(2)}) copy-start(f32[1,2,96,128]{3,2,1,0:T(8,128)} %param.16) | copy-start | bytes 294916
  211.3 51.1 %copy-start.10 = (bf16[1,2,1536]{2,1,0:T(2,128)(2,1)S(1)}, bf16[1,2,1536]{2,1,0:T(2,128)(2,1)}, u32[]{:S(2)}) copy-start(bf16[1,2,1536]{2,1,0:T(2,128)(2,1)} %param.19) | copy-start | bytes 18436
  211.3 150.4 %copy-start.11 = (f32[2,96]{1,0:T(2,128)S(1)}, f32[2,96]{1,0:T(2,128)}, u32[]{:S(2)}) copy-start(f32[2,96]{1,0:T(2,128)} %param.23) | copy-start | bytes 2308
  211.3 150.4 %copy-start.12 = (f32[2,96]{1,0:T(2,128)S(1)}, f32[2,96]{1,0:T(2,128)}, u32[]{:S(2)}) copy-start(f32[2,96]{1,0:T(2,128)} %param.22) | copy-start | bytes 2308
  211.4 269.8 %copy-start.8 = (f32[96,40]{0,1:T(8,128)S(1)}, f32[96,40]{0,1:T(8,128)}, u32[]{:S(2)}) copy-start(f32[96,40]{0,1:T(8,128)} %param.21) | copy-start | bytes 46084
  211.4 269.8 %copy-start.9 = (f32[96,40]{0,1:T(8,128)S(1)}, f32[96,40]{0,1:T(8,128)}, u32[]{:S(2)}) copy-start(f32[96,40]{0,1:T(8,128)} %param.20) | copy-start | bytes 46084
Sparse Core Ops, SparseCore 0:
  12.1 195.7 all-reduce.2
  214.2 266.8 all-reduce.4
  483.9 38.7 all-gather.3
where the time goes:
time: 532 us
  waiting for transfers between devices  317 us (60%)
  blocking collectives  180 us (34%)
  between operations  13.9 us (3%)
  matrix products  10.2 us (2%)
  local copies, waits for them, and re-layouts  5.72 us (1%)
    psum x1, waiting for transfers between devices, per_device(): p_total = lax.psum(p_local, ('shards', 'tensor'))  195 us
    psum x1, waiting for transfers between devices, per_device(): lax.psum((router_term, gain_term), ('shards', 'tensor', 'sections'))  101 us
    psum x1, blocking collectives, per_device(): lax.psum((router_term, gain_term), ('shards', 'tensor', 'sections'))  99.3 us
    psum x1, blocking collectives, per_device(): q_avg = lax.psum(q_local, 'shards') / shard_count  46.7 us
    all_gather x1, waiting for transfers between devices, per_device(): lax.all_gather(weight_rows, 'shards', axis=2, tiled=True)  20.8 us
    all_gather x1, blocking collectives, per_device(): lax.all_gather(router_part, 'shards', axis=0, tiled=True)  17.2 us
    all_gather x1, blocking collectives, per_device(): lax.all_gather(gain_part, 'shards', axis=1, tiled=True)  16.6 us
  transfers between devices with their start and end apart: 3, of which 3 were waited for; matrix products, arithmetic and copies ran while one was open for 2% of the time, Pallas kernels for 0%

commit v1 on v0

v1 whole, which is shorter than its diff:
```python
import jax
import jax.numpy as jnp
from jax import lax
from jax.sharding import PartitionSpec as P

momentum_decay = 0.9
step_size = 0.5
lanes = 128
rank = 32
highest = lax.Precision.HIGHEST
f32 = jnp.float32
plane = ("shards", "tensor")
sheet = ("tensor", "sections")


def exchange(blocks, axes):
    return lax.all_to_all(blocks, axes, 0, 0, tiled=True)


def spread(row, count, axes):
    return exchange(jnp.broadcast_to(row, (count,) + row.shape[1:]), axes)


def per_device(
    replica_grads,
    error_feedback,
    q_start,
    gram_root,
    momentum,
    weights,
    router_partials,
    gain_partials,
    router_momentum,
    router_weights,
    gain_momentum,
    gain_weights,
):
    shard_count = lax.axis_size("shards")
    tensor_count = lax.axis_size("tensor")
    section_count = lax.axis_size("sections")
    plane_count = shard_count * tensor_count
    sheet_count = tensor_count * section_count
    shard_index = lax.axis_index("shards")
    rows = momentum.shape[2]
    width = gain_partials.shape[2]
    start = shard_index * rows
    blocks = width // lanes

    base_rows = weights[0] - (step_size * momentum_decay) * momentum[0]
    base = lax.all_gather(base_rows, "shards", axis=1, tiled=True)

    columns = jnp.concatenate([router_partials[0].T, gain_partials[0]], 0).astype(f32)
    count = columns.shape[0]
    strips = columns.reshape(count, blocks, lanes).transpose(1, 0, 2).reshape(count * blocks, lanes)
    total_rows = plane_count * section_count
    strips = jnp.pad(strips, ((0, total_rows - count * blocks), (0, 0)))
    strips = strips.reshape(tensor_count, section_count, shard_count, lanes).transpose(1, 2, 0, 3)
    strips = strips.reshape(section_count, plane_count, lanes)
    strips = exchange(strips, "sections").sum(0)

    combined = replica_grads[0, 0].astype(f32) + error_feedback[0, 0].astype(f32)
    q_rows = q_start[0].transpose(0, 2, 1)
    p_rows = jnp.einsum("krf,kdf->krd", q_rows, combined, precision=highest)
    p_row = exchange(p_rows.reshape(plane_count, width), plane).sum(0, keepdims=True)
    packed = jnp.concatenate([jnp.broadcast_to(p_row, (plane_count, width)), strips], 1)
    packed = exchange(packed, plane)
    strip = packed[:, width:].sum(0, keepdims=True)
    p_avg = packed[:, :width].reshape(2, rank, width) / shard_count
    p_hat = jnp.einsum("krd,krt->ktd", p_avg, gram_root[0], precision=highest)
    q_local = jnp.einsum("ktd,kdf->ktf", p_hat, combined, precision=highest)

    small_base = jnp.concatenate(
        [
            router_weights.T - (step_size * momentum_decay) * router_momentum.T,
            gain_weights - (step_size * momentum_decay) * gain_momentum,
        ],
        0,
    )
    small_base = jnp.pad(small_base, ((0, 48 - count), (0, lanes - rows)))
    bundle = jnp.concatenate([q_local.reshape(2 * rank, lanes), small_base, jnp.pad(strip, ((0, 7), (0, 0)))], 0)
    bundle = lax.all_gather(bundle, "shards", axis=0, tiled=False)
    q_avg = (bundle[:, : 2 * rank].sum(0) / shard_count).reshape(2, rank, lanes)
    strip_set = bundle[:, 2 * rank + 48]
    small_base = bundle[:, 2 * rank : 2 * rank + count, :rows].transpose(1, 0, 2).reshape(count, width)

    small = spread(strip_set[None], sheet_count, sheet)
    small = small.reshape(total_rows, lanes)[: count * blocks]
    small = small.reshape(blocks, count, lanes).transpose(1, 0, 2).reshape(count, width) / shard_count

    approx = jnp.einsum("ktd,ktf->kdf", p_hat, q_avg, precision=highest)
    new_error = (combined - approx).astype(jnp.bfloat16)[None, None]
    new_weights = (base - step_size * approx)[None]
    approx_rows = lax.dynamic_slice_in_dim(approx, start, rows, 1)
    new_momentum = momentum_decay * momentum + approx_rows[None]

    own = lax.dynamic_slice_in_dim(small, start, rows, 1)
    new_router_momentum = momentum_decay * router_momentum + own[:-2].T
    new_gain_momentum = momentum_decay * gain_momentum + own[-2:]
    new_small = small_base - step_size * small
    return (
        new_error,
        new_momentum,
        new_weights,
        new_router_momentum,
        new_small[:-2].T,
        new_gain_momentum,
        new_small[-2:],
    )


def solution(mesh):
    return jax.shard_map(
        per_device,
        mesh=mesh,
        in_specs=(
            P("shards", "sections", None, None, "tensor"),
            P("shards", "sections", None, None, "tensor"),
            P("sections", None, "tensor", None),
            P("sections", None, None, None),
            P("sections", None, "shards", "tensor"),
            P("sections", None, "shards", "tensor"),
            P(("shards", "tensor", "sections"), None, None),
            P(("shards", "tensor", "sections"), None, None),
            P("shards", None),
            P("shards", None),
            P(None, "shards"),
            P(None, "shards"),
        ),
        out_specs=(
            P("shards", "sections", None, None, "tensor"),
            P("sections", None, "shards", "tensor"),
            P("sections", None, None, "tensor"),
            P("shards", None),
            P(),
            P(None, "shards"),
            P(),
        ),
        check_vma=False,
    )
```

time: 532 us -> 152 us (0.29)
  waiting for transfers between devices: 317 us -> 53.4 us
  blocking collectives: 180 us -> 19.7 us
  starting transfers between devices: 0.12 us -> 35 us
  local copies, waits for them, and re-layouts: 5.72 us -> 14.9 us
    psum x2 -> x0, waiting for transfers between devices: 297 us -> none  [the longest x1 195 us: per_device(): p_total = lax.psum(p_local, ('shards', 'tensor'))]
    psum x2 -> x0, blocking collectives: 146 us -> none  [the longest x1 99.3 us: per_device(): lax.psum((router_term, gain_term), ('shards', 'tensor', 'sections'))]
    all_to_all x0 -> x4, waiting for transfers between devices: none -> 44.6 us  [exchange(): return lax.all_to_all(blocks, axes, 0, 0, tiled=True)]
    all_to_all x0 -> x4, starting transfers between devices: none -> 35 us  [exchange(): return lax.all_to_all(blocks, axes, 0, 0, tiled=True)]
    all_gather x2 -> x1, blocking collectives: 33.8 us -> 19.7 us  [per_device(): bundle = lax.all_gather(bundle, 'shards', axis=0, tiled=False)]
    all_gather x1, waiting for transfers between devices: 20.8 us -> 8.7 us  [per_device(): base = lax.all_gather(base_rows, 'shards', axis=1, tiled=True)]
  transfers between devices with their start and end apart: 3 -> 5, of which waited for: 3 -> 5; matrix products, arithmetic and copies ran while one was open for 2% -> 10% of each run, Pallas kernels for 0% -> 0%
where the time goes in v1:
time: 152 us; the launch traced here: 151 us
  waiting for transfers between devices  53.4 us (35%)
  starting transfers between devices  35 us (23%)
  blocking collectives  19.7 us (13%)
  local copies, waits for them, and re-layouts  14.9 us (10%)
  between operations  14.4 us (9%)
  other arithmetic  7.52 us (5%)
  matrix products  6.02 us (4%)
    all_to_all x4, waiting for transfers between devices, exchange(): return lax.all_to_all(blocks, axes, 0, 0, tiled=True)  44.6 us
    all_to_all x4, starting transfers between devices, exchange(): return lax.all_to_all(blocks, axes, 0, 0, tiled=True)  35 us
    all_gather x1, blocking collectives, per_device(): bundle = lax.all_gather(bundle, 'shards', axis=0, tiled=False)  19.7 us
    all_gather x1, waiting for transfers between devices, per_device(): base = lax.all_gather(base_rows, 'shards', axis=1, tiled=True)  8.7 us
    broadcast_in_dim x1, other arithmetic, per_device(): new_weights = (base - step_size * approx)[None]  3.16 us
  transfers between devices with their start and end apart: 5, of which 5 were waited for; matrix products, arithmetic and copies ran while one was open for 10% of the time, Pallas kernels for 0%

profile of v1, /device:TPU:1, one launch (start us, length us, event | category | flops | bytes accessed | tf_op | source)
XLA Modules:
  0.0 150.9 jit_solution(3413235072184591693)
XLA Ops:
  7.2 0.0 copy-start
  7.2 0.8 concatenate.18
  8.0 1.0 concatenate.17
  9.2 0.8 copy.30
  10.0 7.7 %all-to-all-start.1 = ((f32[8,64,128]{2,1,0:T(8,128)}), f32[8,64,128]{2,1,0:T(8,128)S(1)}, u32[]{:S(2)}, u32[]{:S(2)}) async-start(f32[8,64,128]{2,1,0:T(8,128)} %copy.30), calls=%async_computation.1 | async-start | bytes 524288 | tf_op jit(solution)/shard_map/all_to_all | solution.py:17
  17.6 1.8 %fusion.3 = f32[2,1536,32]{1,2,0:T(8,128)S(1)} fusion(bf16[1,1,2,1536,128]{4,3,2,1,0:T(8,128)(2,1)S(1)} %copy-done.1, bf16[1,1,2,1536,128]{4,3,2,1,0:T(8,128)(2,1)S(1)} %copy-done.2, f32[1,2,128,32]{2,3,1,0:T(8,128)S(1)} %copy-done), kind=kOutput, calls=%fused_computation.5 | convolution fusion | flops 152174592 | bytes 1998848 | tf_op jit(solution)/shard_map/krf,kdf->krd/dot_general | solution.py:63
  19.5 1.2 copy.27
  20.6 6.4 %all-to-all-done.1 = f32[8,64,128]{2,1,0:T(8,128)S(1)} async-done(((f32[8,64,128]{2,1,0:T(8,128)}), f32[8,64,128]{2,1,0:T(8,128)S(1)}, u32[]{:S(2)}, u32[]{:S(2)}) %all-to-all-start.1) | async-done | bytes 262176 | tf_op jit(solution)/shard_map/all_to_all | solution.py:17
  27.0 16.8 %all-to-all-start = ((f32[64,1,1536]{2,1,0:T(1,128)}), f32[64,1,1536]{2,1,0:T(1,128)S(1)}, u32[]{:S(2)}, u32[]{:S(2)}) async-start(f32[64,1,1536]{2,1,0:T(1,128)} %copy.27), calls=%async_computation | async-start | bytes 786432 | tf_op jit(solution)/shard_map/all_to_all | solution.py:17
  43.8 0.0 copy-start.12
  43.8 0.0 copy-start.13
  43.8 0.0 copy-start.9
  43.8 0.0 copy-start.11
  43.9 14.6 %all-to-all-done = f32[64,1,1536]{2,1,0:T(1,128)S(1)} async-done(((f32[64,1,1536]{2,1,0:T(1,128)}), f32[64,1,1536]{2,1,0:T(1,128)S(1)}, u32[]{:S(2)}, u32[]{:S(2)}) %all-to-all-start) | async-done | bytes 393248 | tf_op jit(solution)/shard_map/all_to_all | solution.py:17
  58.4 0.2 reduce_sum.36
  58.7 1.1 all_to_all.23
  59.8 6.0 %all-to-all-start.2 = ((f32[64,1,1664]{2,1,0:T(1,128)}), f32[64,1,1664]{2,1,0:T(1,128)S(1)}, u32[]{:S(2)}, u32[]{:S(2)}) async-start(f32[64,1,1664]{2,1,0:T(1,128)} %all_to_all.23), calls=%async_computation.2 | async-start | bytes 851968 | tf_op jit(solution)/shard_map/all_to_all | solution.py:17
  65.8 0.0 all-gather.4.cloned.1.call-start
  65.9 15.3 %all-to-all-done.2 = f32[64,1,1664]{2,1,0:T(1,128)S(1)} async-done(((f32[64,1,1664]{2,1,0:T(1,128)}), f32[64,1,1664]{2,1,0:T(1,128)S(1)}, u32[]{:S(2)}, u32[]{:S(2)}) %all-to-all-start.2) | async-done | bytes 426016 | tf_op jit(solution)/shard_map/all_to_all | solution.py:17
  81.2 0.5 fusion.7
  81.8 1.1 fusion.1
  82.9 19.7 %all-gather = f32[1920,128]{1,0:T(8,128)S(1)} all-gather(f32[120,128]{1,0:T(8,128)S(1)} %select_maximum_fusion), channel_id=2, replica_groups=mesh['shards'=16,'tensor'=4,'sections'=8] {'shards'}, dimensions={0}, use_global_device_ids=true | all-gather | bytes 1044480 | tf_op jit(solution)/shard_map/all_gather | solution.py:81
  102.6 0.9 copy-done.3
  103.5 2.6 %fusion.11 = f32[2,1536,128]{2,1,0:T(8,128)S(1)} fusion(f32[2,1536,32]{1,2,0:T(8,128)S(1)} %fusion.7, f32[2,32,128]{2,1,0:T(8,128)S(1)} %bitcast.89), kind=kOutput, calls=%fused_computation.36 | convolution fusion | flops 150994944 | bytes 1998848 | tf_op jit(solution)/shard_map/ktd,ktf->kdf/dot_general | solution.py:90
  106.1 0.7 multiply_subtract_fusion
  106.8 0.0 all-gather.4.cloned.1.call-update
  106.8 0.8 slice.43
  107.7 0.7 broadcast_in_dim.31
  108.4 4.6 %all-to-all-start.3 = ((f32[32,16,128]{2,1,0:T(8,128)}), f32[32,16,128]{2,1,0:T(8,128)}, u32[]{:S(2)}, u32[]{:S(2)}) async-start(f32[32,16,128]{2,1,0:T(8,128)} %broadcast_in_dim.31), calls=%async_computation.3 | async-start | bytes 524288 | tf_op jit(solution)/shard_map/all_to_all | solution.py:17
  113.0 1.0 slice.45
  114.0 0.1 copy.43
  114.2 0.9 reshape.78
  115.1 8.4 %all-to-all-done.3 = f32[32,16,128]{2,1,0:T(8,128)} async-done(((f32[32,16,128]{2,1,0:T(8,128)}), f32[32,16,128]{2,1,0:T(8,128)}, u32[]{:S(2)}, u32[]{:S(2)}) %all-to-all-start.3) | async-done | bytes 262176 | tf_op jit(solution)/shard_map/all_to_all | solution.py:17
  123.5 1.8 %slice_multiply_fusion.1 = (f32[504,128]{1,0:T(8,128)}, f32[504,128]{1,0:T(8,128)}) fusion(f32[512,128]{1,0:T(8,128)} %bitcast.22), kind=kLoop, calls=%fused_computation.16 | loop fusion | flops 129024 | bytes 774144 | tf_op jit(solution)/shard_map/mul | solution.py:99
  125.3 1.7 %mul.77 = f32[12,42,128]{2,1,0:T(8,128)} reshape(f32[504,128]{1,0:T(8,128)} %get-tuple-element.9) | data formatting | bytes 516096 | tf_op jit(solution)/shard_map/mul | solution.py:99
  127.0 1.1 copy.34
  128.1 0.1 copy.39
  128.3 0.6 slice.47
  128.9 0.1 copy-done.5
  129.0 1.0 div.36
  129.9 0.0 copy-start.6
  129.9 0.1 copy.32
  130.1 0.1 copy.38
  130.2 0.6 dynamic-slice_add_fusion
  130.8 0.7 fusion.10
  131.5 0.7 slice_bitcast_fusion
  132.2 8.7 %all-gather.4.cloned.1.call-done = f32[1,2,1536,128]{3,2,1,0:T(8,128)} async-done(((f32[1,2,96,128]{3,2,1,0:T(8,128)}), f32[1,2,1536,128]{3,2,1,0:T(8,128)}) %all-gather.4.cloned.1.call-update) | async-done | bytes 1572880 | tf_op jit(solution)/shard_map/all_gather | solution.py:50
  140.9 3.2 %fusion = (f32[1,2,1536,128]{3,2,1,0:T(8,128)}, bf16[1,1,2,1536,128]{4,3,2,1,0:T(8,128)(2,1)}) fusion(f32[1,2,1536,128]{3,2,1,0:T(8,128)} %all-gather.4.cloned.1.call-done, f32[2,1536,128]{2,1,0:T(8,128)S(1)} %fusion.11, bf16[1,1,2,1536,128]{4,3,2,1,0:T(8,128)(2,1)S(1)} %copy-done.1, bf16[1,1,2,1536,128]{4,3,2,1,0:T(8,128)(2,1)S(1)} %copy-done.2), kind=kLoop, calls=%fused_computation.1 | loop fusion | flops 2752512 | bytes 7077888 | tf_op jit(solution)/shard_map/broadcast_in_dim | solution.py:92
  (40 shorter events, 0.5 us)
Async XLA Ops:
  7.2 10.5 %copy-start = (f32[1,2,128,32]{2,3,1,0:T(8,128)S(1)}, f32[1,2,128,32]{2,3,1,0:T(8,128)}, u32[]{:S(2)}) copy-start(f32[1,2,128,32]{2,3,1,0:T(8,128)} %param.14) | copy-start | bytes 98308
  7.2 10.4 %copy-start.1 = (bf16[1,1,2,1536,128]{4,3,2,1,0:T(8,128)(2,1)S(1)}, bf16[1,1,2,1536,128]{4,3,2,1,0:T(8,128)(2,1)}, u32[]{:S(2)}) copy-start(bf16[1,1,2,1536,128]{4,3,2,1,0:T(8,128)(2,1)} %param.13) | copy-start | bytes 2359300
  7.2 10.4 %copy-start.2 = (bf16[1,1,2,1536,128]{4,3,2,1,0:T(8,128)(2,1)S(1)}, bf16[1,1,2,1536,128]{4,3,2,1,0:T(8,128)(2,1)}, u32[]{:S(2)}) copy-start(bf16[1,1,2,1536,128]{4,3,2,1,0:T(8,128)(2,1)} %param.12) | copy-start | bytes 2359300
  10.0 17.1 %all-to-all-start.1 = ((f32[8,64,128]{2,1,0:T(8,128)}), f32[8,64,128]{2,1,0:T(8,128)S(1)}, u32[]{:S(2)}, u32[]{:S(2)}) async-start(f32[8,64,128]{2,1,0:T(8,128)} %copy.30), calls=%async_computation.1 | async-start | bytes 524288 | tf_op jit(solution)/shard_map/all_to_all | solution.py:17
  27.0 31.4 %all-to-all-start = ((f32[64,1,1536]{2,1,0:T(1,128)}), f32[64,1,1536]{2,1,0:T(1,128)S(1)}, u32[]{:S(2)}, u32[]{:S(2)}) async-start(f32[64,1,1536]{2,1,0:T(1,128)} %copy.27), calls=%async_computation | async-start | bytes 786432 | tf_op jit(solution)/shard_map/all_to_all | solution.py:17
  43.8 22.0 %copy-start.12 = (f32[2,96]{1,0:T(2,128)S(1)}, f32[2,96]{1,0:T(2,128)}, u32[]{:S(2)}) copy-start(f32[2,96]{1,0:T(2,128)} %param.22) | copy-start | bytes 2308
  43.8 22.0 %copy-start.13 = (f32[2,96]{1,0:T(2,128)S(1)}, f32[2,96]{1,0:T(2,128)}, u32[]{:S(2)}) copy-start(f32[2,96]{1,0:T(2,128)} %param.23) | copy-start | bytes 2308
  43.8 22.0 %copy-start.9 = (f32[96,40]{0,1:T(8,128)S(1)}, f32[96,40]{0,1:T(8,128)}, u32[]{:S(2)}) copy-start(f32[96,40]{0,1:T(8,128)} %param.20) | copy-start | bytes 46084
  43.8 22.0 %copy-start.11 = (f32[96,40]{0,1:T(8,128)S(1)}, f32[96,40]{0,1:T(8,128)}, u32[]{:S(2)}) copy-start(f32[96,40]{0,1:T(8,128)} %param.21) | copy-start | bytes 46084
  58.7 22.5 %copy-start.10 = (f32[1,2,32,32]{3,2,1,0:T(8,128)S(1)}, f32[1,2,32,32]{3,2,1,0:T(8,128)}, u32[]{:S(2)}) copy-start(f32[1,2,32,32]{3,2,1,0:T(8,128)} %param.15) | copy-start | bytes 24580
  59.8 21.4 %all-to-all-start.2 = ((f32[64,1,1664]{2,1,0:T(1,128)}), f32[64,1,1664]{2,1,0:T(1,128)S(1)}, u32[]{:S(2)}, u32[]{:S(2)}) async-start(f32[64,1,1664]{2,1,0:T(1,128)} %all_to_all.23), calls=%async_computation.2 | async-start | bytes 851968 | tf_op jit(solution)/shard_map/all_to_all | solution.py:17
  65.8 75.2 %all-gather.4.cloned.1.call-start = ((), (), s32[]{:S(2)}) async-start(), calls=%async_computation.4 | async-start | bytes 1671168 | tf_op jit(solution)/shard_map/all_gather | solution.py:50
  102.5 0.9 copy-start.3
  102.5 3.6 %copy-start.7 = (f32[1,2,96,128]{3,2,1,0:T(8,128)S(1)}, f32[1,2,96,128]{3,2,1,0:T(8,128)}, u32[]{:S(2)}) copy-start(f32[1,2,96,128]{3,2,1,0:T(8,128)} %param.17) | copy-start | bytes 294916
  102.5 3.6 %copy-start.8 = (f32[1,2,96,128]{3,2,1,0:T(8,128)S(1)}, f32[1,2,96,128]{3,2,1,0:T(8,128)}, u32[]{:S(2)}) copy-start(f32[1,2,96,128]{3,2,1,0:T(8,128)} %param.16) | copy-start | bytes 294916
  108.4 15.1 %all-to-all-start.3 = ((f32[32,16,128]{2,1,0:T(8,128)}), f32[32,16,128]{2,1,0:T(8,128)}, u32[]{:S(2)}, u32[]{:S(2)}) async-start(f32[32,16,128]{2,1,0:T(8,128)} %broadcast_in_dim.31), calls=%async_computation.3 | async-start | bytes 524288 | tf_op jit(solution)/shard_map/all_to_all | solution.py:17
  123.5 4.7 %copy-start.4 = (f32[42,1536]{1,0:T(8,128)S(1)}, f32[42,1536]{1,0:T(8,128)}, u32[]{:S(2)}) copy-start(f32[42,1536]{1,0:T(8,128)} %reshape.78) | copy-start | bytes 774148
  128.2 0.7 copy-start.5
  129.9 1.6 %copy-start.6 = (f32[42,1536]{1,0:T(8,128)S(1)}, f32[42,1536]{1,0:T(8,128)}, u32[]{:S(2)}) copy-start(f32[42,1536]{1,0:T(8,128)} %copy-done.5) | copy-start | bytes 774148
Sparse Core Ops, SparseCore 0:
  107.0 33.9 all-gather.3

commit v2 on v0

v2 whole, which is shorter than its diff:
```python
import jax
import jax.numpy as jnp
from jax import lax
from jax.experimental import pallas as pl
from jax.experimental.pallas import tpu as pltpu
from jax.sharding import PartitionSpec as P

momentum_decay = 0.9
step_size = 0.5
decayed_step = step_size * momentum_decay
lanes = 128
rank = 32
padded_columns = 48
highest = lax.Precision.HIGHEST
f32 = jnp.float32
plane = ("shards", "tensor")


def exchange(blocks, axes):
    return lax.all_to_all(blocks, axes, 0, 0, tiled=True)


def spread(row, count, axes):
    return exchange(jnp.broadcast_to(row, (count,) + row.shape[1:]), axes)


def prepare_kernel(
    weights, momentum, router_weights, router_momentum, gain_weights, gain_momentum, router, gain, base, strips
):
    rows = weights.shape[0]
    columns, part = router_weights.shape
    gains = gain_weights.shape[0]
    base[:rows] = weights[...] - decayed_step * momentum[...]
    base[rows:] = jnp.zeros((padded_columns, lanes), f32)
    base[rows : rows + columns, :part] = router_weights[...] - decayed_step * router_momentum[...]
    base[rows + columns : rows + columns + gains, :part] = gain_weights[...] - decayed_step * gain_momentum[...]
    blocks = router.shape[1] // lanes
    strips[blocks * (columns + gains) :] = jnp.zeros((strips.shape[0] - blocks * (columns + gains), lanes), f32)
    for i in range(blocks):
        cut = slice(i * lanes, (i + 1) * lanes)
        strips[i * columns : (i + 1) * columns] = router[:, cut].astype(f32)
        row = blocks * columns + i * gains
        strips[row : row + gains] = gain[:, cut].astype(f32)


def finish_kernel(
    index,
    q_set,
    p_hat,
    grads,
    errors,
    base,
    small_base,
    momentum,
    small,
    router_momentum,
    gain_momentum,
    new_error,
    new_momentum,
    new_weights,
    new_router_momentum,
    new_router_weights,
    new_gain_momentum,
    new_gain_weights,
    approx,
    average,
    start,
):
    shards = q_set.shape[0]
    rows = momentum.shape[1]
    q_avg = jnp.sum(q_set[...], 0) / shards
    approx[...] = lax.dot_general(
        p_hat[0], q_avg, (((0,), (0,)), ((), ())), precision=highest, preferred_element_type=f32
    )
    new_error[0] = (grads[0].astype(f32) + errors[0].astype(f32) - approx[...]).astype(jnp.bfloat16)
    new_weights[0] = base[...].reshape(approx.shape) - step_size * approx[...]
    own = pl.ds(pl.multiple_of(index[0] * rows, 8), rows)
    new_momentum[0] = momentum_decay * momentum[0] + approx[own]

    @pl.when(pl.program_id(0) == 0)
    def _():
        columns = router_momentum.shape[0]
        gains = gain_momentum.shape[0]
        blocks = average.shape[1] // lanes
        count = columns + gains
        for i in range(blocks):
            cut = slice(i * lanes, (i + 1) * lanes)
            average[:columns, cut] = small[i * columns : (i + 1) * columns] / shards
            row = blocks * columns + i * gains
            average[columns:count, cut] = small[row : row + gains] / shards
        mine = jnp.zeros((count, rows), f32)
        for i in range(shards):
            cut = slice(i * rows, (i + 1) * rows)
            start[:count, cut] = small_base[i, :count, :rows]
            mine = jnp.where(index[0] == i, average[:count, cut], mine)
        new_router_weights[...] = start[:columns] - step_size * average[:columns]
        new_gain_weights[...] = start[columns:count] - step_size * average[columns:count]
        new_router_momentum[...] = momentum_decay * router_momentum[...] + mine[:columns]
        new_gain_momentum[...] = momentum_decay * gain_momentum[...] + mine[columns:]


def per_device(
    replica_grads,
    error_feedback,
    q_start,
    gram_root,
    momentum,
    weights,
    router_partials,
    gain_partials,
    router_momentum,
    router_weights,
    gain_momentum,
    gain_weights,
):
    shard_count = lax.axis_size("shards")
    section_count = lax.axis_size("sections")
    plane_count = shard_count * lax.axis_size("tensor")
    index = lax.axis_index("shards").astype(jnp.int32)[None]
    pairs, rows = momentum.shape[1:3]
    columns = router_weights.shape[1]
    gains = gain_weights.shape[0]
    width = gain_partials.shape[2]
    held = pairs * rows + padded_columns

    base, strips = pl.pallas_call(
        prepare_kernel,
        out_shape=(
            jax.ShapeDtypeStruct((held, lanes), f32),
            jax.ShapeDtypeStruct((plane_count * section_count, lanes), f32),
        ),
        name="prepare",
    )(
        weights.reshape(pairs * rows, lanes),
        momentum.reshape(pairs * rows, lanes),
        router_weights.T,
        router_momentum.T,
        gain_weights,
        gain_momentum,
        router_partials[0].T,
        gain_partials[0],
    )
    base = lax.all_gather(base, "shards", axis=0, tiled=False)

    strips = exchange(strips.reshape(section_count, plane_count, lanes), "sections").sum(0)
    combined = replica_grads[0, 0].astype(f32) + error_feedback[0, 0].astype(f32)
    q_rows = q_start[0].transpose(0, 2, 1)
    p_rows = jnp.einsum("krf,kdf->krd", q_rows, combined, precision=highest)
    packed = jnp.concatenate([p_rows.reshape(plane_count, width), strips], 1)
    packed = exchange(packed, plane).sum(0, keepdims=True)
    packed = spread(packed, plane_count, plane)
    small = spread(packed[:, width:][None], section_count, "sections")

    p_avg = packed[:, :width].reshape(pairs, rank, width) / shard_count
    p_hat = jnp.einsum("krd,krt->ktd", p_avg, gram_root[0], precision=highest)
    q_local = jnp.einsum("ktd,kdf->ktf", p_hat, combined, precision=highest)
    bundle = q_local.reshape(pairs * rank, lanes)
    bundle, base = lax.optimization_barrier((bundle, base))
    q_set = lax.all_gather(bundle, "shards", axis=0, tiled=False)
    q_set, small = lax.optimization_barrier((q_set, small))

    def whole(*shape):
        return pl.BlockSpec(shape, lambda k, _: (0,) * len(shape))

    def kth(*shape):
        return pl.BlockSpec((1,) + shape, lambda k, _: (k,) + (0,) * len(shape))

    new_error, new_momentum, new_weights, router_step, router_new, gain_step, gain_new = pl.pallas_call(
        finish_kernel,
        grid_spec=pltpu.PrefetchScalarGridSpec(
            num_scalar_prefetch=1,
            grid=(pairs,),
            in_specs=[
                pl.BlockSpec((shard_count, rank, lanes), lambda k, _: (0, k, 0)),
                kth(rank, width),
                kth(width, lanes),
                kth(width, lanes),
                pl.BlockSpec((shard_count, rows, lanes), lambda k, _: (0, k, 0)),
                pl.BlockSpec(
                    (shard_count, padded_columns, lanes), lambda k, _: (0, pairs * rows // padded_columns, 0)
                ),
                kth(rows, lanes),
                whole(plane_count * section_count, lanes),
                whole(columns, rows),
                whole(gains, rows),
            ],
            out_specs=[
                kth(width, lanes),
                kth(rows, lanes),
                kth(width, lanes),
                whole(columns, rows),
                whole(columns, width),
                whole(gains, rows),
                whole(gains, width),
            ],
            scratch_shapes=[
                pltpu.VMEM((width, lanes), f32),
                pltpu.VMEM((padded_columns, width), f32),
                pltpu.VMEM((padded_columns, width), f32),
            ],
        ),
        out_shape=(
            jax.ShapeDtypeStruct((pairs, width, lanes), jnp.bfloat16),
            jax.ShapeDtypeStruct((pairs, rows, lanes), f32),
            jax.ShapeDtypeStruct((pairs, width, lanes), f32),
            jax.ShapeDtypeStruct((columns, rows), f32),
            jax.ShapeDtypeStruct((columns, width), f32),
            jax.ShapeDtypeStruct((gains, rows), f32),
            jax.ShapeDtypeStruct((gains, width), f32),
        ),
        name="finish",
    )(
        index,
        q_set,
        p_hat,
        replica_grads[0, 0],
        error_feedback[0, 0],
        base,
        base,
        momentum[0],
        small.reshape(plane_count * section_count, lanes),
        router_momentum.T,
        gain_momentum,
    )
    return (
        new_error[None, None],
        new_momentum[None],
        new_weights[None],
        router_step.T,
        router_new.T,
        gain_step,
        gain_new,
    )


def solution(mesh):
    return jax.shard_map(
        per_device,
        mesh=mesh,
        in_specs=(
            P("shards", "sections", None, None, "tensor"),
            P("shards", "sections", None, None, "tensor"),
            P("sections", None, "tensor", None),
            P("sections", None, None, None),
            P("sections", None, "shards", "tensor"),
            P("sections", None, "shards", "tensor"),
            P(("shards", "tensor", "sections"), None, None),
            P(("shards", "tensor", "sections"), None, None),
            P("shards", None),
            P("shards", None),
            P(None, "shards"),
            P(None, "shards"),
        ),
        out_specs=(
            P("shards", "sections", None, None, "tensor"),
            P("sections", None, "shards", "tensor"),
            P("sections", None, None, "tensor"),
            P("shards", None),
            P(),
            P(None, "shards"),
            P(),
        ),
        check_vma=False,
    )
```

time: 532 us -> 124 us (0.23)
  waiting for transfers between devices: 317 us -> 21.6 us
  blocking collectives: 180 us -> 54.6 us
  starting transfers between devices: 0.12 us -> 17.3 us
  Pallas kernels: 0 us -> 7.55 us
  matrix products: 10.2 us -> 4.76 us
    psum x2 -> x0, waiting for transfers between devices: 297 us -> none  [the longest x1 195 us: per_device(): p_total = lax.psum(p_local, ('shards', 'tensor'))]
    psum x2 -> x0, blocking collectives: 146 us -> none  [the longest x1 99.3 us: per_device(): lax.psum((router_term, gain_term), ('shards', 'tensor', 'sections'))]
    all_to_all x0 -> x1, blocking collectives: none -> 34.9 us  [exchange(): return lax.all_to_all(blocks, axes, 0, 0, tiled=True)]
    all_to_all x0 -> x3, waiting for transfers between devices: none -> 21.5 us  [exchange(): return lax.all_to_all(blocks, axes, 0, 0, tiled=True)]
    all_gather x1, waiting for transfers between devices: 20.8 us -> 0.02 us  [per_device(): base = lax.all_gather(base, 'shards', axis=0, tiled=False)]
    all_to_all x0 -> x3, starting transfers between devices: none -> 17.3 us  [exchange(): return lax.all_to_all(blocks, axes, 0, 0, tiled=True)]
    all_gather x2 -> x1, blocking collectives: 33.8 us -> 19.7 us  [per_device(): q_set = lax.all_gather(bundle, 'shards', axis=0, tiled=False)]
    pallas_call x0 -> x2, Pallas kernels: none -> 7.55 us  [the longest x1 5.72 us: per_device(): pl.pallas_call(finish_kernel, grid_spec=pltpu.PrefetchScalarGridSpec(num_...]
  transfers between devices with their start and end apart: 3 -> 4, of which waited for: 3 -> 2; matrix products, arithmetic and copies ran while one was open for 2% -> 6% of each run, Pallas kernels for 0% -> 0%
where the time goes in v2:
time: 124 us; the launch traced here: 123 us
  blocking collectives  54.6 us (44%)
  waiting for transfers between devices  21.6 us (17%)
  starting transfers between devices  17.3 us (14%)
  between operations  14.2 us (11%)
  Pallas kernels  7.55 us (6%)
  matrix products  4.76 us (4%)
  local copies, waits for them, and re-layouts  2.77 us (2%)
    all_to_all x1, blocking collectives, exchange(): return lax.all_to_all(blocks, axes, 0, 0, tiled=True)  34.9 us
    all_to_all x3, waiting for transfers between devices, exchange(): return lax.all_to_all(blocks, axes, 0, 0, tiled=True)  21.5 us
    all_gather x1, blocking collectives, per_device(): q_set = lax.all_gather(bundle, 'shards', axis=0, tiled=False)  19.7 us
    all_to_all x3, starting transfers between devices, exchange(): return lax.all_to_all(blocks, axes, 0, 0, tiled=True)  17.3 us
    pallas_call x1, Pallas kernels, per_device(): pl.pallas_call(finish_kernel, grid_spec=pltpu.PrefetchScalarGridSpec(num_...  5.72 us
    dot_general x1, matrix products, per_device(): p_rows = jnp.einsum('krf,kdf->krd', q_rows, combined, precision=highest)  3.17 us
  transfers between devices with their start and end apart: 4, of which 2 were waited for; matrix products, arithmetic and copies ran while one was open for 6% of the time, Pallas kernels for 0%

profile of v2, /device:TPU:1, one launch (start us, length us, event | category | flops | bytes accessed | tf_op | source)
XLA Modules:
  0.0 123.1 jit_solution(13746862677115281090)
XLA Ops:
  7.2 0.0 copy-start
  7.2 0.0 all-gather.4.cloned.1.call-start
  7.2 1.8 %prepare.1 = (f32[240,128]{1,0:T(8,128)}, f32[512,128]{1,0:T(8,128)}) custom-call(f32[192,128]{1,0:T(8,128)} %bitcast.70, f32[192,128]{1,0:T(8,128)} %bitcast.65, f32[40,96]{1,0:T(8,128)} %bitcast.73, f32[40,96]{1,0:T(8,128)} %bitcast.71, f32[2,96]{1,0:T(2,128)} %gain_weights.1, f32[2,96]{1,0:T(2,128)} %gain_momentum.3, bf16[40,1536]{1,0:T(8,128)(2,1)} %bitcast.69, ...), custom_call_target="tpu_custom_call" | custom-call | tf_op jit(solution)/shard_map/prepare/pallas_call | solution.py:126
  9.1 0.0 all-gather.4.cloned.1.call-update
  9.1 7.7 %all-to-all-start = ((f32[8,64,128]{2,1,0:T(8,128)}), f32[8,64,128]{2,1,0:T(8,128)S(1)}, u32[]{:S(2)}, u32[]{:S(2)}) async-start(f32[8,64,128]{2,1,0:T(8,128)} %bitcast.67), calls=%async_computation | async-start | bytes 524288 | tf_op jit(solution)/shard_map/all_to_all | solution.py:20
  16.7 0.0 copy-done
  16.8 3.2 %fusion.1 = f32[2,1536,32]{1,2,0:T(8,128)S(1)} fusion(f32[1,2,128,32]{2,3,1,0:T(8,128)S(1)} %copy-done, bf16[1,1,2,1536,128]{4,3,2,1,0:T(8,128)(2,1)} %param.13, bf16[1,1,2,1536,128]{4,3,2,1,0:T(8,128)(2,1)} %param.12), kind=kOutput, calls=%fused_computation.2 | convolution fusion | flops 152174592 | bytes 1998848 | tf_op jit(solution)/shard_map/krf,kdf->krd/dot_general | solution.py:148
  19.9 6.2 %all-to-all-done = f32[8,64,128]{2,1,0:T(8,128)S(1)} async-done(((f32[8,64,128]{2,1,0:T(8,128)}), f32[8,64,128]{2,1,0:T(8,128)S(1)}, u32[]{:S(2)}, u32[]{:S(2)}) %all-to-all-start) | async-done | bytes 262176 | tf_op jit(solution)/shard_map/all_to_all | solution.py:20
  26.2 0.3 all_to_all.19
  26.5 34.9 %all_to_all.28 = f32[64,1,1664]{2,1,0:T(1,128)S(1)} all-to-all(f32[64,1,1664]{2,1,0:T(1,128)S(1)} %all_to_all.19), channel_id=1, replica_groups=mesh['shards'=16,'tensor'=4,'sections'=8] {'shards','tensor'}, dimensions={0} | all-to-all | bytes 851968 | tf_op jit(solution)/shard_map/all_to_all | solution.py:20
  61.4 0.3 reduce_sum.19
  61.7 1.0 broadcast_in_dim.25
  62.6 0.0 copy-start.5
  62.6 6.2 %all-to-all-start.2 = ((f32[64,1,1664]{2,1,0:T(1,128)}), f32[64,1,1664]{2,1,0:T(1,128)S(1)}, u32[]{:S(2)}, u32[]{:S(2)}) async-start(f32[64,1,1664]{2,1,0:T(1,128)} %broadcast_in_dim.25), calls=%async_computation.2 | async-start | bytes 851968 | tf_op jit(solution)/shard_map/all_to_all | solution.py:20
  68.9 0.0 copy-start.1
  68.9 0.0 copy-start.2
  68.9 15.3 %all-to-all-done.2 = f32[64,1,1664]{2,1,0:T(1,128)S(1)} async-done(((f32[64,1,1664]{2,1,0:T(1,128)}), f32[64,1,1664]{2,1,0:T(1,128)S(1)}, u32[]{:S(2)}, u32[]{:S(2)}) %all-to-all-start.2) | async-done | bytes 426016 | tf_op jit(solution)/shard_map/all_to_all | solution.py:20
  84.2 0.7 broadcast_in_dim.26
  85.0 3.4 %all-to-all-start.3 = ((f32[8,64,128]{2,1,0:T(8,128)}), f32[8,64,128]{2,1,0:T(8,128)S(1)}, u32[]{:S(2)}, u32[]{:S(2)}) async-start(f32[8,64,128]{2,1,0:T(8,128)} %broadcast_in_dim.26), calls=%async_computation.3 | async-start | bytes 524288 | tf_op jit(solution)/shard_map/all_to_all | solution.py:20
  88.4 0.0 copy-done.5
  88.4 0.5 fusion.2
  89.0 0.0 copy-done.1
  89.0 0.0 copy-done.2
  89.0 0.0 copy-start.3
  89.0 1.1 fusion
  90.1 0.0 all-gather.4.cloned.1.call-done
  90.1 19.7 %all-gather.1 = f32[1024,128]{1,0:T(8,128)} all-gather(f32[64,128]{1,0:T(8,128)S(1)} %bitcast.68), channel_id=3, replica_groups=mesh['shards'=16,'tensor'=4,'sections'=8] {'shards'}, dimensions={0}, use_global_device_ids=true | all-gather | bytes 557056 | tf_op jit(solution)/shard_map/all_gather | solution.py:159
  109.8 0.0 all-to-all-done.3
  109.8 0.0 copy-start.4
  109.8 0.0 copy-done.3
  109.8 0.7 copy-done.4
  110.5 5.7 %finish.1 = (bf16[2,1536,128]{2,1,0:T(8,128)(2,1)}, f32[2,96,128]{2,1,0:T(8,128)}, f32[2,1536,128]{2,1,0:T(8,128)}, f32[40,96]{1,0:T(8,128)}, f32[40,1536]{1,0:T...) custom-call(s32[1]{0:T(128)} %bitcast.index, f32[16,64,128]{2,1,0:T(8,128)} %bitcast.59, f32[2,32,1536]{2,1,0:T(8,128)} %bitcast.58, ...), custom_call_target="tpu_custom_call" | custom-call | tf_op jit(solution)/shard_map/finish/pallas_call | solution.py:168
  (5 shorter events, 0.1 us)
Async XLA Ops:
  7.2 9.6 %copy-start = (f32[1,2,128,32]{2,3,1,0:T(8,128)S(1)}, f32[1,2,128,32]{2,3,1,0:T(8,128)}, u32[]{:S(2)}) copy-start(f32[1,2,128,32]{2,3,1,0:T(8,128)} %param.14) | copy-start | bytes 98308
  7.2 82.9 %all-gather.4.cloned.1.call-start = ((), (), s32[]{:S(2)}) async-start(), calls=%async_computation.4 | async-start | bytes 2088960 | tf_op jit(solution)/shard_map/all_gather | solution.py:143
  9.1 17.1 %all-to-all-start = ((f32[8,64,128]{2,1,0:T(8,128)}), f32[8,64,128]{2,1,0:T(8,128)S(1)}, u32[]{:S(2)}, u32[]{:S(2)}) async-start(f32[8,64,128]{2,1,0:T(8,128)} %bitcast.67), calls=%async_computation | async-start | bytes 524288 | tf_op jit(solution)/shard_map/all_to_all | solution.py:20
  62.6 25.8 %copy-start.5 = (f32[1,2,32,32]{3,2,1,0:T(8,128)S(1)}, f32[1,2,32,32]{3,2,1,0:T(8,128)}, u32[]{:S(2)}) copy-start(f32[1,2,32,32]{3,2,1,0:T(8,128)} %param.15) | copy-start | bytes 24580
  62.6 21.5 %all-to-all-start.2 = ((f32[64,1,1664]{2,1,0:T(1,128)}), f32[64,1,1664]{2,1,0:T(1,128)S(1)}, u32[]{:S(2)}, u32[]{:S(2)}) async-start(f32[64,1,1664]{2,1,0:T(1,128)} %broadcast_in_dim.25), calls=%async_computation.2 | async-start | bytes 851968 | tf_op jit(solution)/shard_map/all_to_all | solution.py:20
  68.9 20.1 %copy-start.1 = (bf16[1,1,2,1536,128]{4,3,2,1,0:T(8,128)(2,1)S(1)}, bf16[1,1,2,1536,128]{4,3,2,1,0:T(8,128)(2,1)}, u32[]{:S(2)}) copy-start(bf16[1,1,2,1536,128]{4,3,2,1,0:T(8,128)(2,1)} %param.13) | copy-start | bytes 2359300
  68.9 20.1 %copy-start.2 = (bf16[1,1,2,1536,128]{4,3,2,1,0:T(8,128)(2,1)S(1)}, bf16[1,1,2,1536,128]{4,3,2,1,0:T(8,128)(2,1)}, u32[]{:S(2)}) copy-start(bf16[1,1,2,1536,128]{4,3,2,1,0:T(8,128)(2,1)} %param.12) | copy-start | bytes 2359300
  85.0 24.8 %all-to-all-start.3 = ((f32[8,64,128]{2,1,0:T(8,128)}), f32[8,64,128]{2,1,0:T(8,128)S(1)}, u32[]{:S(2)}, u32[]{:S(2)}) async-start(f32[8,64,128]{2,1,0:T(8,128)} %broadcast_in_dim.26), calls=%async_computation.3 | async-start | bytes 524288 | tf_op jit(solution)/shard_map/all_to_all | solution.py:20
  89.0 20.8 %copy-start.3 = (f32[2,1536,32]{1,2,0:T(8,128)}, f32[2,1536,32]{1,2,0:T(8,128)S(1)}, u32[]{:S(2)}) copy-start(f32[2,1536,32]{1,2,0:T(8,128)S(1)} %fusion.2) | copy-start | bytes 1179652
  109.8 0.7 copy-start.4
Sparse Core Ops, SparseCore 0:
  10.7 51.6 all-gather.3

commit v3 on v2

--- a/solution.py
+++ b/solution.py
@@ -3,6 +3,7 @@
 from jax import lax
 from jax.experimental import pallas as pl
 from jax.experimental.pallas import tpu as pltpu
+from jax.sharding import Mesh
 from jax.sharding import PartitionSpec as P
 
 momentum_decay = 0.9
@@ -13,7 +14,8 @@
 padded_columns = 48
 highest = lax.Precision.HIGHEST
 f32 = jnp.float32
-plane = ("shards", "tensor")
+shards = ("stack", "core")
+layer = ("stack", "tensor")
 
 
 def exchange(blocks, axes):
@@ -41,6 +43,13 @@
         strips[i * columns : (i + 1) * columns] = router[:, cut].astype(f32)
         row = blocks * columns + i * gains
         strips[row : row + gains] = gain[:, cut].astype(f32)
+
+
+def pieces(value):
+    high = value.astype(jnp.bfloat16)
+    rest = value - high.astype(f32)
+    mid = rest.astype(jnp.bfloat16)
+    return high, mid, (rest - mid.astype(f32)).astype(jnp.bfloat16)
 
 
 def finish_kernel(
@@ -69,9 +78,11 @@
     shards = q_set.shape[0]
     rows = momentum.shape[1]
     q_avg = jnp.sum(q_set[...], 0) / shards
-    approx[...] = lax.dot_general(
-        p_hat[0], q_avg, (((0,), (0,)), ((), ())), precision=highest, preferred_element_type=f32
-    )
+    p_high, p_mid, p_low = pieces(p_hat[0])
+    q_high, q_mid, q_low = pieces(q_avg)
+    left = jnp.concatenate([p_high, p_high, p_high, p_mid, p_mid, p_low], 0)
+    right = jnp.concatenate([q_high, q_mid, q_low, q_high, q_mid, q_high], 0)
+    approx[...] = lax.dot_general(left, right, (((0,), (0,)), ((), ())), preferred_element_type=f32)
     new_error[0] = (grads[0].astype(f32) + errors[0].astype(f32) - approx[...]).astype(jnp.bfloat16)
     new_weights[0] = base[...].reshape(approx.shape) - step_size * approx[...]
     own = pl.ds(pl.multiple_of(index[0] * rows, 8), rows)
@@ -113,10 +124,12 @@
     gain_momentum,
     gain_weights,
 ):
-    shard_count = lax.axis_size("shards")
+    shard_count = lax.axis_size(shards)
     section_count = lax.axis_size("sections")
-    plane_count = shard_count * lax.axis_size("tensor")
-    index = lax.axis_index("shards").astype(jnp.int32)[None]
+    layer_count = lax.axis_size(layer)
+    strip_count = 2 * layer_count
+    core = lax.axis_index("core")
+    index = lax.axis_index(shards).astype(jnp.int32)[None]
     pairs, rows = momentum.shape[1:3]
     columns = router_weights.shape[1]
     gains = gain_weights.shape[0]
@@ -127,7 +140,7 @@
         prepare_kernel,
         out_shape=(
             jax.ShapeDtypeStruct((held, lanes), f32),
-            jax.ShapeDtypeStruct((plane_count * section_count, lanes), f32),
+            jax.ShapeDtypeStruct((strip_count * section_count, lanes), f32),
         ),
         name="prepare",
     )(
@@ -140,23 +153,29 @@
         router_partials[0].T,
         gain_partials[0],
     )
-    base = lax.all_gather(base, "shards", axis=0, tiled=False)
-
-    strips = exchange(strips.reshape(section_count, plane_count, lanes), "sections").sum(0)
+    base = lax.all_gather(base, shards, axis=0, tiled=False)
+
+    strips = exchange(strips.reshape(section_count, strip_count, lanes), "sections").sum(0)
     combined = replica_grads[0, 0].astype(f32) + error_feedback[0, 0].astype(f32)
     q_rows = q_start[0].transpose(0, 2, 1)
     p_rows = jnp.einsum("krf,kdf->krd", q_rows, combined, precision=highest)
-    packed = jnp.concatenate([p_rows.reshape(plane_count, width), strips], 1)
-    packed = exchange(packed, plane).sum(0, keepdims=True)
-    packed = spread(packed, plane_count, plane)
-    small = spread(packed[:, width:][None], section_count, "sections")
-
-    p_avg = packed[:, :width].reshape(pairs, rank, width) / shard_count
+    kept = lax.dynamic_index_in_dim(p_rows, core, 0, keepdims=False)
+    sent = lax.dynamic_index_in_dim(p_rows, 1 - core, 0, keepdims=False)
+    sent = lax.all_gather(sent, "core", axis=0, tiled=False)
+    p_rows = kept + lax.dynamic_index_in_dim(sent, 1 - core, 0, keepdims=False)
+    packed = jnp.concatenate([p_rows, strips.reshape(layer_count, 2 * lanes)], 1)
+    packed = exchange(packed, layer).sum(0, keepdims=True)
+    packed = spread(packed, layer_count, layer)
+    packed = lax.all_gather(packed, "core", axis=0, tiled=False)
+    strips = packed[:, :, width:].sum(0).reshape(1, strip_count, lanes)
+    small = spread(strips, section_count, "sections")
+
+    p_avg = packed[:, :, :width] / shard_count
     p_hat = jnp.einsum("krd,krt->ktd", p_avg, gram_root[0], precision=highest)
     q_local = jnp.einsum("ktd,kdf->ktf", p_hat, combined, precision=highest)
     bundle = q_local.reshape(pairs * rank, lanes)
     bundle, base = lax.optimization_barrier((bundle, base))
-    q_set = lax.all_gather(bundle, "shards", axis=0, tiled=False)
+    q_set = lax.all_gather(bundle, shards, axis=0, tiled=False)
     q_set, small = lax.optimization_barrier((q_set, small))
 
     def whole(*shape):
@@ -180,7 +199,7 @@
                     (shard_count, padded_columns, lanes), lambda k, _: (0, pairs * rows // padded_columns, 0)
                 ),
                 kth(rows, lanes),
-                whole(plane_count * section_count, lanes),
+                whole(strip_count * section_count, lanes),
                 whole(columns, rows),
                 whole(gains, rows),
             ],
@@ -218,7 +237,7 @@
         base,
         base,
         momentum[0],
-        small.reshape(plane_count * section_count, lanes),
+        small.reshape(strip_count * section_count, lanes),
         router_momentum.T,
         gain_momentum,
     )
@@ -234,30 +253,32 @@
 
 
 def solution(mesh):
+    count, *others = mesh.devices.shape
+    split = Mesh(mesh.devices.reshape(count // 2, 2, *others), ("stack", "core", "tensor", "sections"))
     return jax.shard_map(
         per_device,
-        mesh=mesh,
+        mesh=split,
         in_specs=(
-            P("shards", "sections", None, None, "tensor"),
-            P("shards", "sections", None, None, "tensor"),
+            P(shards, "sections", None, None, "tensor"),
+            P(shards, "sections", None, None, "tensor"),
             P("sections", None, "tensor", None),
             P("sections", None, None, None),
-            P("sections", None, "shards", "tensor"),
-            P("sections", None, "shards", "tensor"),
-            P(("shards", "tensor", "sections"), None, None),
-            P(("shards", "tensor", "sections"), None, None),
-            P("shards", None),
-            P("shards", None),
-            P(None, "shards"),
-            P(None, "shards"),
+            P("sections", None, shards, "tensor"),
+            P("sections", None, shards, "tensor"),
+            P(("stack", "core", "tensor", "sections"), None, None),
+            P(("stack", "core", "tensor", "sections"), None, None),
+            P(shards, None),
+            P(shards, None),
+            P(None, shards),
+            P(None, shards),
         ),
         out_specs=(
-            P("shards", "sections", None, None, "tensor"),
-            P("sections", None, "shards", "tensor"),
+            P(shards, "sections", None, None, "tensor"),
+            P("sections", None, shards, "tensor"),
             P("sections", None, None, "tensor"),
-            P("shards", None),
+            P(shards, None),
             P(),
-            P(None, "shards"),
+            P(None, shards),
             P(),
         ),
         check_vma=False,

time: 124 us -> 111 us (0.90)
  waiting for transfers between devices: 21.6 us -> 11.9 us
  blocking collectives: 54.6 us -> 52.8 us
    all_to_all x1, blocking collectives: 34.9 us -> 24.1 us  [exchange(): return lax.all_to_all(blocks, axes, 0, 0, tiled=True)]
    all_to_all x3, waiting for transfers between devices: 21.5 us -> 11.9 us  [exchange(): return lax.all_to_all(blocks, axes, 0, 0, tiled=True)]
    all_gather x1 -> x3, blocking collectives: 19.7 us -> 28.7 us  [the longest x1 18.2 us: per_device(): q_set = lax.all_gather(bundle, shards, axis=0, tiled=False)]
where the time goes in v3:
time: 111 us; the launch traced here: 110 us
  blocking collectives  52.8 us (48%)
  starting transfers between devices  17.2 us (15%)
  between operations  14.2 us (13%)
  waiting for transfers between devices  11.9 us (11%)
  Pallas kernels  6.76 us (6%)
  matrix products  4.76 us (4%)
  local copies, waits for them, and re-layouts  2.57 us (2%)
    all_to_all x1, blocking collectives, exchange(): return lax.all_to_all(blocks, axes, 0, 0, tiled=True)  24.1 us
    all_gather x1, blocking collectives, per_device(): q_set = lax.all_gather(bundle, shards, axis=0, tiled=False)  18.2 us
    all_to_all x3, starting transfers between devices, exchange(): return lax.all_to_all(blocks, axes, 0, 0, tiled=True)  17.1 us
    all_to_all x3, waiting for transfers between devices, exchange(): return lax.all_to_all(blocks, axes, 0, 0, tiled=True)  11.9 us
    all_gather x1, blocking collectives, per_device(): packed = lax.all_gather(packed, 'core', axis=0, tiled=False)  6.18 us
    pallas_call x1, Pallas kernels, per_device(): pl.pallas_call(finish_kernel, grid_spec=pltpu.PrefetchScalarGridSpec(num_...  4.93 us
    all_gather x1, blocking collectives, per_device(): sent = lax.all_gather(sent, 'core', axis=0, tiled=False)  4.38 us
    dot_general x1, matrix products, per_device(): p_rows = jnp.einsum('krf,kdf->krd', q_rows, combined, precision=highest)  3.17 us
  transfers between devices with their start and end apart: 4, of which 2 were waited for; matrix products, arithmetic and copies ran while one was open for 6% of the time, Pallas kernels for 0%

profile of v3, /device:TPU:1, one launch (start us, length us, event | category | flops | bytes accessed | tf_op | source)
XLA Modules:
  0.0 110.5 jit_solution(7600902623501811718)
XLA Ops:
  7.2 0.0 copy-start
  7.2 0.0 all-gather.5.cloned.1.call-start
  7.2 1.8 %prepare.1 = (f32[240,128]{1,0:T(8,128)}, f32[512,128]{1,0:T(8,128)}) custom-call(f32[192,128]{1,0:T(8,128)} %bitcast.71, f32[192,128]{1,0:T(8,128)} %bitcast.66, f32[40,96]{1,0:T(8,128)} %bitcast.74, f32[40,96]{1,0:T(8,128)} %bitcast.72, f32[2,96]{1,0:T(2,128)} %gain_weights.1, f32[2,96]{1,0:T(2,128)} %gain_momentum.3, bf16[40,1536]{1,0:T(8,128)(2,1)} %bitcast.70, ...), custom_call_target="tpu_custom_call" | custom-call | tf_op jit(solution)/shard_map/prepare/pallas_call | solution.py:139
  9.1 0.0 all-gather.5.cloned.1.call-update
  9.1 7.7 %all-to-all-start = ((f32[8,64,128]{2,1,0:T(8,128)}), f32[8,64,128]{2,1,0:T(8,128)S(1)}, u32[]{:S(2)}, u32[]{:S(2)}) async-start(f32[8,64,128]{2,1,0:T(8,128)} %bitcast.68), calls=%async_computation | async-start | bytes 524288 | tf_op jit(solution)/shard_map/all_to_all | solution.py:22
  16.7 0.0 copy-done
  16.8 3.2 %fusion.1 = f32[2,1536,32]{1,2,0:T(8,128)S(1)} fusion(f32[1,2,128,32]{2,3,1,0:T(8,128)S(1)} %copy-done, bf16[1,1,2,1536,128]{4,3,2,1,0:T(8,128)(2,1)} %param.13, bf16[1,1,2,1536,128]{4,3,2,1,0:T(8,128)(2,1)} %param.12), kind=kOutput, calls=%fused_computation.2 | convolution fusion | flops 152174592 | bytes 1998848 | tf_op jit(solution)/shard_map/krf,kdf->krd/dot_general | solution.py:161
  20.0 4.4 %all_gather.22 = f32[2,32,1536]{2,1,0:T(8,128)S(1)} all-gather(f32[1,32,1536]{2,1,0:T(8,128)S(1)} %dynamic-slice_bitcast_fusion), channel_id=1, replica_groups=mesh['stack'=8,'core'=2,'tensor'=4,'sections'=8] {'core'}, dimensions={0}, use_global_device_ids=true | all-gather | bytes 589824 | tf_op jit(solution)/shard_map/all_gather | solution.py:164
  24.4 1.8 %all-to-all-done = f32[8,64,128]{2,1,0:T(8,128)S(1)} async-done(((f32[8,64,128]{2,1,0:T(8,128)}), f32[8,64,128]{2,1,0:T(8,128)S(1)}, u32[]{:S(2)}, u32[]{:S(2)}) %all-to-all-start) | async-done | bytes 262176 | tf_op jit(solution)/shard_map/all_to_all | solution.py:22
  26.2 0.2 copy.22
  26.5 24.1 %all_to_all.25 = f32[32,1,1792]{2,1,0:T(1,128)S(1)} all-to-all(f32[32,1,1792]{2,1,0:T(1,128)S(1)} %copy.22), channel_id=1, replica_groups=mesh['stack'=8,'core'=2,'tensor'=4,'sections'=8] {'stack','tensor'}, dimensions={0} | all-to-all | bytes 458752 | tf_op jit(solution)/shard_map/all_to_all | solution.py:22
  50.6 0.1 reduce_sum.28
  50.7 0.8 broadcast_in_dim.26
  51.5 0.0 copy-start.5
  51.5 6.1 %all-to-all-start.2 = ((f32[32,1,1792]{2,1,0:T(1,128)}), f32[32,1,1792]{2,1,0:T(1,128)S(1)}, u32[]{:S(2)}, u32[]{:S(2)}) async-start(f32[32,1,1792]{2,1,0:T(1,128)} %broadcast_in_dim.26), calls=%async_computation.2 | async-start | bytes 458752 | tf_op jit(solution)/shard_map/all_to_all | solution.py:22
  57.6 0.0 copy-start.1
  57.6 0.0 copy-start.2
  57.6 10.1 %all-to-all-done.2 = f32[32,1,1792]{2,1,0:T(1,128)S(1)} async-done(((f32[32,1,1792]{2,1,0:T(1,128)}), f32[32,1,1792]{2,1,0:T(1,128)S(1)}, u32[]{:S(2)}, u32[]{:S(2)}) %all-to-all-start.2) | async-done | bytes 229408 | tf_op jit(solution)/shard_map/all_to_all | solution.py:22
  67.7 6.2 %all-gather = f32[64,1,1792]{2,1,0:T(1,128)S(1)} all-gather(f32[32,1,1792]{2,1,0:T(1,128)S(1)} %all-to-all-done.2), channel_id=2, replica_groups=mesh['stack'=8,'core'=2,'tensor'=4,'sections'=8] {'core'}, dimensions={0}, use_global_device_ids=true | all-gather | bytes 688128 | tf_op jit(solution)/shard_map/all_gather | solution.py:169
  74.0 0.7 broadcast_in_dim.28
  74.7 3.4 %all-to-all-start.3 = ((f32[8,64,128]{2,1,0:T(8,128)}), f32[8,64,128]{2,1,0:T(8,128)S(1)}, u32[]{:S(2)}, u32[]{:S(2)}) async-start(f32[8,64,128]{2,1,0:T(8,128)} %broadcast_in_dim.28), calls=%async_computation.3 | async-start | bytes 524288 | tf_op jit(solution)/shard_map/all_to_all | solution.py:22
  78.1 0.0 copy-done.5
  78.1 0.5 fusion.2
  78.7 0.0 copy-done.1
  78.7 0.0 copy-done.2
  78.7 0.0 copy-start.3
  78.7 1.1 fusion
  79.8 0.0 all-gather.5.cloned.1.call-done
  79.8 18.2 %all-gather.2 = f32[1024,128]{1,0:T(8,128)} all-gather(f32[64,128]{1,0:T(8,128)S(1)} %bitcast.69), channel_id=4, replica_groups=mesh['stack'=8,'core'=2,'tensor'=4,'sections'=8] {'stack','core'}, dimensions={0}, use_global_device_ids=true | all-gather | bytes 557056 | tf_op jit(solution)/shard_map/all_gather | solution.py:178
  98.0 0.0 all-to-all-done.3
  98.0 0.0 copy-start.4
  98.0 0.0 copy-done.3
  98.0 0.7 copy-done.4
  98.7 4.9 %finish.1 = (bf16[2,1536,128]{2,1,0:T(8,128)(2,1)}, f32[2,96,128]{2,1,0:T(8,128)}, f32[2,1536,128]{2,1,0:T(8,128)}, f32[40,96]{1,0:T(8,128)}, f32[40,1536]{1,0:T...) custom-call(s32[1]{0:T(128)} %bitcast.index, f32[16,64,128]{2,1,0:T(8,128)} %bitcast.62, f32[2,32,1536]{2,1,0:T(8,128)} %bitcast.61, ...), custom_call_target="tpu_custom_call" | custom-call | tf_op jit(solution)/shard_map/finish/pallas_call | solution.py:187
  (8 shorter events, 0.1 us)
Async XLA Ops:
  7.2 9.6 %copy-start = (f32[1,2,128,32]{2,3,1,0:T(8,128)S(1)}, f32[1,2,128,32]{2,3,1,0:T(8,128)}, u32[]{:S(2)}) copy-start(f32[1,2,128,32]{2,3,1,0:T(8,128)} %param.14) | copy-start | bytes 98308
  7.2 72.6 %all-gather.5.cloned.1.call-start = ((), (), s32[]{:S(2)}) async-start(), calls=%async_computation.4 | async-start | bytes 2088960 | tf_op jit(solution)/shard_map/all_gather | solution.py:156
  9.1 17.1 %all-to-all-start = ((f32[8,64,128]{2,1,0:T(8,128)}), f32[8,64,128]{2,1,0:T(8,128)S(1)}, u32[]{:S(2)}, u32[]{:S(2)}) async-start(f32[8,64,128]{2,1,0:T(8,128)} %bitcast.68), calls=%async_computation | async-start | bytes 524288 | tf_op jit(solution)/shard_map/all_to_all | solution.py:22
  51.5 26.6 %copy-start.5 = (f32[1,2,32,32]{3,2,1,0:T(8,128)S(1)}, f32[1,2,32,32]{3,2,1,0:T(8,128)}, u32[]{:S(2)}) copy-start(f32[1,2,32,32]{3,2,1,0:T(8,128)} %param.15) | copy-start | bytes 24580
  51.5 16.2 %all-to-all-start.2 = ((f32[32,1,1792]{2,1,0:T(1,128)}), f32[32,1,1792]{2,1,0:T(1,128)S(1)}, u32[]{:S(2)}, u32[]{:S(2)}) async-start(f32[32,1,1792]{2,1,0:T(1,128)} %broadcast_in_dim.26), calls=%async_computation.2 | async-start | bytes 458752 | tf_op jit(solution)/shard_map/all_to_all | solution.py:22
  57.6 21.0 %copy-start.1 = (bf16[1,1,2,1536,128]{4,3,2,1,0:T(8,128)(2,1)S(1)}, bf16[1,1,2,1536,128]{4,3,2,1,0:T(8,128)(2,1)}, u32[]{:S(2)}) copy-start(bf16[1,1,2,1536,128]{4,3,2,1,0:T(8,128)(2,1)} %param.13) | copy-start | bytes 2359300
  57.6 21.0 %copy-start.2 = (bf16[1,1,2,1536,128]{4,3,2,1,0:T(8,128)(2,1)S(1)}, bf16[1,1,2,1536,128]{4,3,2,1,0:T(8,128)(2,1)}, u32[]{:S(2)}) copy-start(bf16[1,1,2,1536,128]{4,3,2,1,0:T(8,128)(2,1)} %param.12) | copy-start | bytes 2359300
  74.7 23.3 %all-to-all-start.3 = ((f32[8,64,128]{2,1,0:T(8,128)}), f32[8,64,128]{2,1,0:T(8,128)S(1)}, u32[]{:S(2)}, u32[]{:S(2)}) async-start(f32[8,64,128]{2,1,0:T(8,128)} %broadcast_in_dim.28), calls=%async_computation.3 | async-start | bytes 524288 | tf_op jit(solution)/shard_map/all_to_all | solution.py:22
  78.7 19.3 %copy-start.3 = (f32[2,1536,32]{1,2,0:T(8,128)}, f32[2,1536,32]{1,2,0:T(8,128)S(1)}, u32[]{:S(2)}) copy-start(f32[2,1536,32]{1,2,0:T(8,128)S(1)} %fusion.2) | copy-start | bytes 1179652
  98.0 0.7 copy-start.4
Sparse Core Ops, SparseCore 0:
  10.7 49.4 all-gather.4

commit v4 on v3

--- a/solution.py
+++ b/solution.py
@@ -12,6 +12,7 @@
 lanes = 128
 rank = 32
 padded_columns = 48
+finish_vmem = 51 << 20
 highest = lax.Precision.HIGHEST
 f32 = jnp.float32
 shards = ("stack", "core")
@@ -227,6 +228,7 @@
             jax.ShapeDtypeStruct((gains, rows), f32),
             jax.ShapeDtypeStruct((gains, width), f32),
         ),
+        compiler_params=pltpu.CompilerParams(vmem_limit_bytes=finish_vmem),
         name="finish",
     )(
         index,

time: 111 us -> 108 us (0.973)
  blocking collectives: 52.8 us -> 51.4 us
    all_gather x1, blocking collectives: 18.2 us -> 16.8 us  [per_device(): q_set = lax.all_gather(bundle, shards, axis=0, tiled=False)]
where the time goes in v4:
time: 108 us
  blocking collectives  51.4 us (48%)
  starting transfers between devices  17.2 us (16%)
  between operations  14.2 us (13%)
  waiting for transfers between devices  11.9 us (11%)
  Pallas kernels  6.28 us (6%)
  matrix products  4.75 us (4%)
  local copies, waits for them, and re-layouts  1.88 us (2%)
    all_to_all x1, blocking collectives, exchange(): return lax.all_to_all(blocks, axes, 0, 0, tiled=True)  24.1 us
    all_to_all x3, starting transfers between devices, exchange(): return lax.all_to_all(blocks, axes, 0, 0, tiled=True)  17.1 us
    all_gather x1, blocking collectives, per_device(): q_set = lax.all_gather(bundle, shards, axis=0, tiled=False)  16.8 us
    all_to_all x3, waiting for transfers between devices, exchange(): return lax.all_to_all(blocks, axes, 0, 0, tiled=True)  11.9 us
    all_gather x1, blocking collectives, per_device(): packed = lax.all_gather(packed, 'core', axis=0, tiled=False)  6.18 us
    pallas_call x1, Pallas kernels, per_device(): pl.pallas_call(finish_kernel, grid_spec=pltpu.PrefetchScalarGridSpec(num_...  4.45 us
    all_gather x1, blocking collectives, per_device(): sent = lax.all_gather(sent, 'core', axis=0, tiled=False)  4.38 us
    dot_general x1, matrix products, per_device(): p_rows = jnp.einsum('krf,kdf->krd', q_rows, combined, precision=highest)  3.17 us
  transfers between devices with their start and end apart: 4, of which 2 were waited for; matrix products, arithmetic and copies ran while one was open for 6% of the time, Pallas kernels for 0%

profile of v4, /device:TPU:1, one launch (start us, length us, event | category | flops | bytes accessed | tf_op | source)
XLA Modules:
  0.0 107.9 jit_solution(5059840666578554090)
XLA Ops:
  7.2 0.0 copy-start
  7.2 0.0 all-gather.5.cloned.1.call-start
  7.2 1.8 %prepare.1 = (f32[240,128]{1,0:T(8,128)}, f32[512,128]{1,0:T(8,128)}) custom-call(f32[192,128]{1,0:T(8,128)} %bitcast.73, f32[192,128]{1,0:T(8,128)} %bitcast.62, f32[40,96]{1,0:T(8,128)} %bitcast.74, f32[40,96]{1,0:T(8,128)} %bitcast.64, f32[2,96]{1,0:T(2,128)} %gain_weights.1, f32[2,96]{1,0:T(2,128)} %gain_momentum.3, bf16[40,1536]{1,0:T(8,128)(2,1)} %bitcast.72, ...), custom_call_target="tpu_custom_call" | custom-call | tf_op jit(solution)/shard_map/prepare/pallas_call | solution.py:140
  9.1 0.0 all-gather.5.cloned.1.call-update
  9.1 7.7 %all-to-all-start = ((f32[8,64,128]{2,1,0:T(8,128)}), f32[8,64,128]{2,1,0:T(8,128)S(1)}, u32[]{:S(2)}, u32[]{:S(2)}) async-start(f32[8,64,128]{2,1,0:T(8,128)} %bitcast.70), calls=%async_computation | async-start | bytes 524288 | tf_op jit(solution)/shard_map/all_to_all | solution.py:23
  16.7 0.0 copy-done
  16.8 3.2 %fusion.1 = f32[2,1536,32]{1,2,0:T(8,128)S(1)} fusion(f32[1,2,128,32]{2,3,1,0:T(8,128)S(1)} %copy-done, bf16[1,1,2,1536,128]{4,3,2,1,0:T(8,128)(2,1)} %param.13, bf16[1,1,2,1536,128]{4,3,2,1,0:T(8,128)(2,1)} %param.12), kind=kOutput, calls=%fused_computation.2 | convolution fusion | flops 152174592 | bytes 1998848 | tf_op jit(solution)/shard_map/krf,kdf->krd/dot_general | solution.py:162
  20.0 4.4 %all_gather.22 = f32[2,32,1536]{2,1,0:T(8,128)S(1)} all-gather(f32[1,32,1536]{2,1,0:T(8,128)S(1)} %dynamic-slice_bitcast_fusion), channel_id=1, replica_groups=mesh['stack'=8,'core'=2,'tensor'=4,'sections'=8] {'core'}, dimensions={0}, use_global_device_ids=true | all-gather | bytes 589824 | tf_op jit(solution)/shard_map/all_gather | solution.py:165
  24.4 1.8 %all-to-all-done = f32[8,64,128]{2,1,0:T(8,128)S(1)} async-done(((f32[8,64,128]{2,1,0:T(8,128)}), f32[8,64,128]{2,1,0:T(8,128)S(1)}, u32[]{:S(2)}, u32[]{:S(2)}) %all-to-all-start) | async-done | bytes 262176 | tf_op jit(solution)/shard_map/all_to_all | solution.py:23
  26.2 0.2 copy.22
  26.5 24.1 %all_to_all.25 = f32[32,1,1792]{2,1,0:T(1,128)S(1)} all-to-all(f32[32,1,1792]{2,1,0:T(1,128)S(1)} %copy.22), channel_id=1, replica_groups=mesh['stack'=8,'core'=2,'tensor'=4,'sections'=8] {'stack','tensor'}, dimensions={0} | all-to-all | bytes 458752 | tf_op jit(solution)/shard_map/all_to_all | solution.py:23
  50.6 0.1 reduce_sum.28
  50.7 0.8 broadcast_in_dim.26
  51.5 0.0 copy-start.6
  51.5 6.1 %all-to-all-start.2 = ((f32[32,1,1792]{2,1,0:T(1,128)}), f32[32,1,1792]{2,1,0:T(1,128)S(1)}, u32[]{:S(2)}, u32[]{:S(2)}) async-start(f32[32,1,1792]{2,1,0:T(1,128)} %broadcast_in_dim.26), calls=%async_computation.2 | async-start | bytes 458752 | tf_op jit(solution)/shard_map/all_to_all | solution.py:23
  57.6 0.0 copy-start.1
  57.6 0.0 copy-start.2
  57.6 10.1 %all-to-all-done.2 = f32[32,1,1792]{2,1,0:T(1,128)S(1)} async-done(((f32[32,1,1792]{2,1,0:T(1,128)}), f32[32,1,1792]{2,1,0:T(1,128)S(1)}, u32[]{:S(2)}, u32[]{:S(2)}) %all-to-all-start.2) | async-done | bytes 229408 | tf_op jit(solution)/shard_map/all_to_all | solution.py:23
  67.7 6.2 %all-gather = f32[64,1,1792]{2,1,0:T(1,128)S(1)} all-gather(f32[32,1,1792]{2,1,0:T(1,128)S(1)} %all-to-all-done.2), channel_id=2, replica_groups=mesh['stack'=8,'core'=2,'tensor'=4,'sections'=8] {'core'}, dimensions={0}, use_global_device_ids=true | all-gather | bytes 688128 | tf_op jit(solution)/shard_map/all_gather | solution.py:170
  74.0 0.7 broadcast_in_dim.28
  74.7 3.4 %all-to-all-start.3 = ((f32[8,64,128]{2,1,0:T(8,128)}), f32[8,64,128]{2,1,0:T(8,128)S(1)}, u32[]{:S(2)}, u32[]{:S(2)}) async-start(f32[8,64,128]{2,1,0:T(8,128)} %broadcast_in_dim.28), calls=%async_computation.3 | async-start | bytes 524288 | tf_op jit(solution)/shard_map/all_to_all | solution.py:23
  78.1 0.0 copy-done.6
  78.1 0.0 copy-start.3
  78.1 0.0 copy-start.4
  78.2 0.0 copy-start.5
  78.2 0.5 fusion.2
  78.7 0.0 copy-done.1
  78.7 0.0 copy-done.2
  78.7 1.1 fusion
  79.8 0.0 all-gather.5.cloned.1.call-done
  79.8 16.8 %all-gather.2 = f32[1024,128]{1,0:T(8,128)S(1)} all-gather(f32[64,128]{1,0:T(8,128)S(1)} %bitcast.71), channel_id=4, replica_groups=mesh['stack'=8,'core'=2,'tensor'=4,'sections'=8] {'stack','core'}, dimensions={0}, use_global_device_ids=true | all-gather | bytes 557056 | tf_op jit(solution)/shard_map/all_gather | solution.py:179
  96.6 0.0 all-to-all-done.3
  96.6 0.0 copy-done.3
  96.6 0.0 copy-done.4
  96.6 0.0 copy-done.5
  96.6 4.4 %finish.1 = (bf16[2,1536,128]{2,1,0:T(8,128)(2,1)}, f32[2,96,128]{2,1,0:T(8,128)}, f32[2,1536,128]{2,1,0:T(8,128)}, f32[40,96]{1,0:T(8,128)}, f32[40,1536]{1,0:T...) custom-call(s32[1]{0:T(128)} %bitcast.index, f32[16,64,128]{2,1,0:T(8,128)S(1)} %bitcast.60, f32[2,32,1536]{2,1,0:T(8,128)S(1)} %bitcast.59, ...), custom_call_target="tpu_custom_call" | custom-call | tf_op jit(solution)/shard_map/finish/pallas_call | solution.py:188
  (8 shorter events, 0.1 us)
Async XLA Ops:
  7.2 9.6 %copy-start = (f32[1,2,128,32]{2,3,1,0:T(8,128)S(1)}, f32[1,2,128,32]{2,3,1,0:T(8,128)}, u32[]{:S(2)}) copy-start(f32[1,2,128,32]{2,3,1,0:T(8,128)} %param.14) | copy-start | bytes 98308
  7.2 72.6 %all-gather.5.cloned.1.call-start = ((), (), s32[]{:S(2)}) async-start(), calls=%async_computation.4 | async-start | bytes 2088960 | tf_op jit(solution)/shard_map/all_gather | solution.py:157
  9.1 17.1 %all-to-all-start = ((f32[8,64,128]{2,1,0:T(8,128)}), f32[8,64,128]{2,1,0:T(8,128)S(1)}, u32[]{:S(2)}, u32[]{:S(2)}) async-start(f32[8,64,128]{2,1,0:T(8,128)} %bitcast.70), calls=%async_computation | async-start | bytes 524288 | tf_op jit(solution)/shard_map/all_to_all | solution.py:23
  51.5 26.6 %copy-start.6 = (f32[1,2,32,32]{3,2,1,0:T(8,128)S(1)}, f32[1,2,32,32]{3,2,1,0:T(8,128)}, u32[]{:S(2)}) copy-start(f32[1,2,32,32]{3,2,1,0:T(8,128)} %param.15) | copy-start | bytes 24580
  51.5 16.2 %all-to-all-start.2 = ((f32[32,1,1792]{2,1,0:T(1,128)}), f32[32,1,1792]{2,1,0:T(1,128)S(1)}, u32[]{:S(2)}, u32[]{:S(2)}) async-start(f32[32,1,1792]{2,1,0:T(1,128)} %broadcast_in_dim.26), calls=%async_computation.2 | async-start | bytes 458752 | tf_op jit(solution)/shard_map/all_to_all | solution.py:23
  57.6 21.1 %copy-start.1 = (bf16[1,1,2,1536,128]{4,3,2,1,0:T(8,128)(2,1)S(1)}, bf16[1,1,2,1536,128]{4,3,2,1,0:T(8,128)(2,1)}, u32[]{:S(2)}) copy-start(bf16[1,1,2,1536,128]{4,3,2,1,0:T(8,128)(2,1)} %param.13) | copy-start | bytes 2359300
  57.6 21.1 %copy-start.2 = (bf16[1,1,2,1536,128]{4,3,2,1,0:T(8,128)(2,1)S(1)}, bf16[1,1,2,1536,128]{4,3,2,1,0:T(8,128)(2,1)}, u32[]{:S(2)}) copy-start(bf16[1,1,2,1536,128]{4,3,2,1,0:T(8,128)(2,1)} %param.12) | copy-start | bytes 2359300
  74.7 21.9 %all-to-all-start.3 = ((f32[8,64,128]{2,1,0:T(8,128)}), f32[8,64,128]{2,1,0:T(8,128)S(1)}, u32[]{:S(2)}, u32[]{:S(2)}) async-start(f32[8,64,128]{2,1,0:T(8,128)} %broadcast_in_dim.28), calls=%async_computation.3 | async-start | bytes 524288 | tf_op jit(solution)/shard_map/all_to_all | solution.py:23
  78.1 18.5 %copy-start.3 = (f32[1,2,96,128]{3,2,1,0:T(8,128)S(1)}, f32[1,2,96,128]{3,2,1,0:T(8,128)}, u32[]{:S(2)}) copy-start(f32[1,2,96,128]{3,2,1,0:T(8,128)} %param.16) | copy-start | bytes 294916
  78.1 18.5 %copy-start.4 = (f32[96,40]{0,1:T(8,128)S(1)}, f32[96,40]{0,1:T(8,128)}, u32[]{:S(2)}) copy-start(f32[96,40]{0,1:T(8,128)} %param.20) | copy-start | bytes 46084
  78.2 18.4 %copy-start.5 = (f32[2,96]{1,0:T(2,128)S(1)}, f32[2,96]{1,0:T(2,128)}, u32[]{:S(2)}) copy-start(f32[2,96]{1,0:T(2,128)} %gain_momentum.3) | copy-start | bytes 2308
Sparse Core Ops, SparseCore 0:
  10.7 49.4 all-gather.4

commit v5 on v4

--- a/solution.py
+++ b/solution.py
@@ -100,15 +100,17 @@
             average[:columns, cut] = small[i * columns : (i + 1) * columns] / shards
             row = blocks * columns + i * gains
             average[columns:count, cut] = small[row : row + gains] / shards
-        mine = jnp.zeros((count, rows), f32)
         for i in range(shards):
             cut = slice(i * rows, (i + 1) * rows)
             start[:count, cut] = small_base[i, :count, :rows]
-            mine = jnp.where(index[0] == i, average[:count, cut], mine)
+
+            @pl.when(index[0] == i)
+            def _():
+                new_router_momentum[...] = momentum_decay * router_momentum[...] + average[:columns, cut]
+                new_gain_momentum[...] = momentum_decay * gain_momentum[...] + average[columns:count, cut]
+
         new_router_weights[...] = start[:columns] - step_size * average[:columns]
         new_gain_weights[...] = start[columns:count] - step_size * average[columns:count]
-        new_router_momentum[...] = momentum_decay * router_momentum[...] + mine[:columns]
-        new_gain_momentum[...] = momentum_decay * gain_momentum[...] + mine[columns:]
 
 
 def per_device(
@@ -159,7 +161,12 @@
     strips = exchange(strips.reshape(section_count, strip_count, lanes), "sections").sum(0)
     combined = replica_grads[0, 0].astype(f32) + error_feedback[0, 0].astype(f32)
     q_rows = q_start[0].transpose(0, 2, 1)
-    p_rows = jnp.einsum("krf,kdf->krd", q_rows, combined, precision=highest)
+    q_high = lax.reduce_precision(q_rows, 8, 7)
+    q_mid = lax.reduce_precision(q_rows - q_high, 8, 7)
+    q_set = jnp.concatenate([q_high, q_mid, q_rows - q_high - q_mid], 1).astype(jnp.bfloat16)
+    p_set = jnp.einsum("krf,kdf->krd", q_set, replica_grads[0, 0], preferred_element_type=f32)
+    p_set += jnp.einsum("krf,kdf->krd", q_set, error_feedback[0, 0], preferred_element_type=f32)
+    p_rows = p_set.reshape(pairs, 3, rank, width).sum(1)
     kept = lax.dynamic_index_in_dim(p_rows, core, 0, keepdims=False)
     sent = lax.dynamic_index_in_dim(p_rows, 1 - core, 0, keepdims=False)
     sent = lax.all_gather(sent, "core", axis=0, tiled=False)

time: 108 us -> 108 us (level)
  matrix products: 4.75 us -> 2.35 us
  waiting for transfers between devices: 11.9 us -> 13.5 us
    dot_general x1 -> x2, matrix products: 3.17 us -> 0.77 us  [the longest x1 0.39 us: per_device(): jnp.einsum('krf,kdf->krd', q_set, error_feedback[0, 0], preferred_element...]
    all_to_all x3, waiting for transfers between devices: 11.9 us -> 13.5 us  [exchange(): return lax.all_to_all(blocks, axes, 0, 0, tiled=True)]
  transfers between devices with their start and end apart: 4 -> 4, of which waited for: 2 -> 2; matrix products, arithmetic and copies ran while one was open for 6% -> 5% of each run, Pallas kernels for 0% -> 0%
where the time goes in v5:
time: 108 us
  blocking collectives  51.8 us (48%)
  starting transfers between devices  16.5 us (15%)
  between operations  14.2 us (13%)
  waiting for transfers between devices  13.5 us (12%)
  Pallas kernels  6.24 us (6%)
  matrix products  2.35 us (2%)
  local copies, waits for them, and re-layouts  1.87 us (2%)
    all_to_all x1, blocking collectives, exchange(): return lax.all_to_all(blocks, axes, 0, 0, tiled=True)  24.6 us
    all_gather x1, blocking collectives, per_device(): q_set = lax.all_gather(bundle, shards, axis=0, tiled=False)  16.8 us
    all_to_all x3, starting transfers between devices, exchange(): return lax.all_to_all(blocks, axes, 0, 0, tiled=True)  16.5 us
    all_to_all x3, waiting for transfers between devices, exchange(): return lax.all_to_all(blocks, axes, 0, 0, tiled=True)  13.5 us
    all_gather x1, blocking collectives, per_device(): packed = lax.all_gather(packed, 'core', axis=0, tiled=False)  6.04 us
    all_gather x1, blocking collectives, per_device(): sent = lax.all_gather(sent, 'core', axis=0, tiled=False)  4.37 us
    pallas_call x1, Pallas kernels, per_device(): pl.pallas_call(finish_kernel, grid_spec=pltpu.PrefetchScalarGridSpec(num_...  4.3 us
  transfers between devices with their start and end apart: 4, of which 2 were waited for; matrix products, arithmetic and copies ran while one was open for 5% of the time, Pallas kernels for 0%

profile of v5, /device:TPU:1, one launch (start us, length us, event | category | flops | bytes accessed | tf_op | source)
XLA Modules:
  0.0 107.5 jit_solution(9517647592738296501)
XLA Ops:
  7.2 0.0 copy-start
  7.2 0.0 copy-start.1
  7.2 0.0 all-gather.5.cloned.1.call-start
  7.2 0.0 copy-start.2
  7.2 1.9 %prepare.1 = (f32[240,128]{1,0:T(8,128)}, f32[512,128]{1,0:T(8,128)}) custom-call(f32[192,128]{1,0:T(8,128)} %bitcast.71, f32[192,128]{1,0:T(8,128)} %bitcast.59, f32[40,96]{1,0:T(8,128)} %bitcast.72, f32[40,96]{1,0:T(8,128)} %bitcast.61, f32[2,96]{1,0:T(2,128)} %gain_weights.1, f32[2,96]{1,0:T(2,128)} %gain_momentum.3, bf16[40,1536]{1,0:T(8,128)(2,1)} %bitcast.70, ...), custom_call_target="tpu_custom_call" | custom-call | tf_op jit(solution)/shard_map/prepare/pallas_call | solution.py:142
  9.2 0.0 all-gather.5.cloned.1.call-update
  9.2 7.7 %all-to-all-start = ((f32[8,64,128]{2,1,0:T(8,128)}), f32[8,64,128]{2,1,0:T(8,128)S(1)}, u32[]{:S(2)}, u32[]{:S(2)}) async-start(f32[8,64,128]{2,1,0:T(8,128)} %bitcast.68), calls=%async_computation | async-start | bytes 524288 | tf_op jit(solution)/shard_map/all_to_all | solution.py:23
  16.9 0.8 reduce-precision_convert_fusion.1
  17.6 0.0 copy-done.1
  17.7 0.4 fusion.8
  18.0 0.0 copy-done.2
  18.0 0.4 convolution_add_fusion
  18.4 0.1 reduce_sum.36
  18.6 4.4 %all_gather.22 = f32[2,32,1536]{2,1,0:T(8,128)S(1)} all-gather(f32[1,32,1536]{2,1,0:T(8,128)S(1)} %constant_dynamic-slice_fusion), channel_id=1, replica_groups=mesh['stack'=8,'core'=2,'tensor'=4,'sections'=8] {'core'}, dimensions={0}, use_global_device_ids=true | all-gather | bytes 589824 | tf_op jit(solution)/shard_map/all_gather | solution.py:172
  23.0 3.3 %all-to-all-done = f32[8,64,128]{2,1,0:T(8,128)S(1)} async-done(((f32[8,64,128]{2,1,0:T(8,128)}), f32[8,64,128]{2,1,0:T(8,128)S(1)}, u32[]{:S(2)}, u32[]{:S(2)}) %all-to-all-start) | async-done | bytes 262176 | tf_op jit(solution)/shard_map/all_to_all | solution.py:23
  26.3 0.2 copy.22
  26.6 24.6 %all_to_all.25 = f32[32,1,1792]{2,1,0:T(1,128)S(1)} all-to-all(f32[32,1,1792]{2,1,0:T(1,128)S(1)} %copy.22), channel_id=1, replica_groups=mesh['stack'=8,'core'=2,'tensor'=4,'sections'=8] {'stack','tensor'}, dimensions={0} | all-to-all | bytes 458752 | tf_op jit(solution)/shard_map/all_to_all | solution.py:23
  51.2 0.1 reduce_sum.38
  51.3 0.8 broadcast_in_dim.26
  52.1 5.4 %all-to-all-start.2 = ((f32[32,1,1792]{2,1,0:T(1,128)}), f32[32,1,1792]{2,1,0:T(1,128)S(1)}, u32[]{:S(2)}, u32[]{:S(2)}) async-start(f32[32,1,1792]{2,1,0:T(1,128)} %broadcast_in_dim.26), calls=%async_computation.2 | async-start | bytes 458752 | tf_op jit(solution)/shard_map/all_to_all | solution.py:23
  57.5 10.1 %all-to-all-done.2 = f32[32,1,1792]{2,1,0:T(1,128)S(1)} async-done(((f32[32,1,1792]{2,1,0:T(1,128)}), f32[32,1,1792]{2,1,0:T(1,128)S(1)}, u32[]{:S(2)}, u32[]{:S(2)}) %all-to-all-start.2) | async-done | bytes 229408 | tf_op jit(solution)/shard_map/all_to_all | solution.py:23
  67.7 6.0 %all-gather = f32[64,1,1792]{2,1,0:T(1,128)S(1)} all-gather(f32[32,1,1792]{2,1,0:T(1,128)S(1)} %all-to-all-done.2), channel_id=2, replica_groups=mesh['stack'=8,'core'=2,'tensor'=4,'sections'=8] {'core'}, dimensions={0}, use_global_device_ids=true | all-gather | bytes 688128 | tf_op jit(solution)/shard_map/all_gather | solution.py:177
  73.8 0.7 broadcast_in_dim.28
  74.5 3.4 %all-to-all-start.3 = ((f32[8,64,128]{2,1,0:T(8,128)}), f32[8,64,128]{2,1,0:T(8,128)S(1)}, u32[]{:S(2)}, u32[]{:S(2)}) async-start(f32[8,64,128]{2,1,0:T(8,128)} %broadcast_in_dim.28), calls=%async_computation.3 | async-start | bytes 524288 | tf_op jit(solution)/shard_map/all_to_all | solution.py:23
  77.9 0.0 copy-done
  77.9 0.0 copy-start.3
  77.9 0.0 copy-start.4
  77.9 0.0 copy-start.5
  77.9 0.5 fusion.4
  78.5 1.1 fusion
  79.5 0.0 all-gather.5.cloned.1.call-done
  79.6 16.8 %all-gather.2 = f32[1024,128]{1,0:T(8,128)S(1)} all-gather(f32[64,128]{1,0:T(8,128)S(1)} %bitcast.69), channel_id=4, replica_groups=mesh['stack'=8,'core'=2,'tensor'=4,'sections'=8] {'stack','core'}, dimensions={0}, use_global_device_ids=true | all-gather | bytes 557056 | tf_op jit(solution)/shard_map/all_gather | solution.py:186
  96.3 0.0 all-to-all-done.3
  96.3 0.0 copy-done.3
  96.4 0.0 copy-done.4
  96.4 0.0 copy-done.5
  96.4 4.3 %finish.1 = (bf16[2,1536,128]{2,1,0:T(8,128)(2,1)}, f32[2,96,128]{2,1,0:T(8,128)}, f32[2,1536,128]{2,1,0:T(8,128)}, f32[40,96]{1,0:T(8,128)}, f32[40,1536]{1,0:T...) custom-call(s32[1]{0:T(128)} %bitcast.index, f32[16,64,128]{2,1,0:T(8,128)S(1)} %bitcast.57, f32[2,32,1536]{2,1,0:T(8,128)S(1)} %bitcast.56, ...), custom_call_target="tpu_custom_call" | custom-call | tf_op jit(solution)/shard_map/finish/pallas_call | solution.py:195
  (8 shorter events, 0.1 us)
Async XLA Ops:
  7.2 70.7 %copy-start = (f32[1,2,32,32]{3,2,1,0:T(8,128)S(1)}, f32[1,2,32,32]{3,2,1,0:T(8,128)}, u32[]{:S(2)}) copy-start(f32[1,2,32,32]{3,2,1,0:T(8,128)} %param.15) | copy-start | bytes 24580
  7.2 10.5 %copy-start.1 = (bf16[1,1,2,1536,128]{4,3,2,1,0:T(8,128)(2,1)S(1)}, bf16[1,1,2,1536,128]{4,3,2,1,0:T(8,128)(2,1)}, u32[]{:S(2)}) copy-start(bf16[1,1,2,1536,128]{4,3,2,1,0:T(8,128)(2,1)} %param.12) | copy-start | bytes 2359300
  7.2 72.4 %all-gather.5.cloned.1.call-start = ((), (), s32[]{:S(2)}) async-start(), calls=%async_computation.4 | async-start | bytes 2088960 | tf_op jit(solution)/shard_map/all_gather | solution.py:159
  7.2 10.8 %copy-start.2 = (bf16[1,1,2,1536,128]{4,3,2,1,0:T(8,128)(2,1)S(1)}, bf16[1,1,2,1536,128]{4,3,2,1,0:T(8,128)(2,1)}, u32[]{:S(2)}) copy-start(bf16[1,1,2,1536,128]{4,3,2,1,0:T(8,128)(2,1)} %param.13) | copy-start | bytes 2359300
  9.2 17.1 %all-to-all-start = ((f32[8,64,128]{2,1,0:T(8,128)}), f32[8,64,128]{2,1,0:T(8,128)S(1)}, u32[]{:S(2)}, u32[]{:S(2)}) async-start(f32[8,64,128]{2,1,0:T(8,128)} %bitcast.68), calls=%async_computation | async-start | bytes 524288 | tf_op jit(solution)/shard_map/all_to_all | solution.py:23
  52.1 15.5 %all-to-all-start.2 = ((f32[32,1,1792]{2,1,0:T(1,128)}), f32[32,1,1792]{2,1,0:T(1,128)S(1)}, u32[]{:S(2)}, u32[]{:S(2)}) async-start(f32[32,1,1792]{2,1,0:T(1,128)} %broadcast_in_dim.26), calls=%async_computation.2 | async-start | bytes 458752 | tf_op jit(solution)/shard_map/all_to_all | solution.py:23
  74.5 21.9 %all-to-all-start.3 = ((f32[8,64,128]{2,1,0:T(8,128)}), f32[8,64,128]{2,1,0:T(8,128)S(1)}, u32[]{:S(2)}, u32[]{:S(2)}) async-start(f32[8,64,128]{2,1,0:T(8,128)} %broadcast_in_dim.28), calls=%async_computation.3 | async-start | bytes 524288 | tf_op jit(solution)/shard_map/all_to_all | solution.py:23
  77.9 18.4 %copy-start.3 = (f32[1,2,96,128]{3,2,1,0:T(8,128)S(1)}, f32[1,2,96,128]{3,2,1,0:T(8,128)}, u32[]{:S(2)}) copy-start(f32[1,2,96,128]{3,2,1,0:T(8,128)} %param.16) | copy-start | bytes 294916
  77.9 18.4 %copy-start.4 = (f32[96,40]{0,1:T(8,128)S(1)}, f32[96,40]{0,1:T(8,128)}, u32[]{:S(2)}) copy-start(f32[96,40]{0,1:T(8,128)} %param.20) | copy-start | bytes 46084
  77.9 18.4 %copy-start.5 = (f32[2,96]{1,0:T(2,128)S(1)}, f32[2,96]{1,0:T(2,128)}, u32[]{:S(2)}) copy-start(f32[2,96]{1,0:T(2,128)} %gain_momentum.3) | copy-start | bytes 2308
Sparse Core Ops, SparseCore 0:
  10.7 49.3 all-gather.4

commit v6 on v5

--- a/solution.py
+++ b/solution.py
@@ -12,7 +12,7 @@
 lanes = 128
 rank = 32
 padded_columns = 48
-finish_vmem = 51 << 20
+finish_vmem = 24 << 20
 highest = lax.Precision.HIGHEST
 f32 = jnp.float32
 shards = ("stack", "core")
@@ -85,7 +85,7 @@
     right = jnp.concatenate([q_high, q_mid, q_low, q_high, q_mid, q_high], 0)
     approx[...] = lax.dot_general(left, right, (((0,), (0,)), ((), ())), preferred_element_type=f32)
     new_error[0] = (grads[0].astype(f32) + errors[0].astype(f32) - approx[...]).astype(jnp.bfloat16)
-    new_weights[0] = base[...].reshape(approx.shape) - step_size * approx[...]
+    new_weights[0] = 0.5 * base[...].reshape(approx.shape) - step_size * approx[...]
     own = pl.ds(pl.multiple_of(index[0] * rows, 8), rows)
     new_momentum[0] = momentum_decay * momentum[0] + approx[own]
 
@@ -102,7 +102,7 @@
             average[columns:count, cut] = small[row : row + gains] / shards
         for i in range(shards):
             cut = slice(i * rows, (i + 1) * rows)
-            start[:count, cut] = small_base[i, :count, :rows]
+            start[:count, cut] = 0.5 * small_base[i, :count, :rows]
 
             @pl.when(index[0] == i)
             def _():
@@ -174,6 +174,7 @@
     packed = jnp.concatenate([p_rows, strips.reshape(layer_count, 2 * lanes)], 1)
     packed = exchange(packed, layer).sum(0, keepdims=True)
     packed = spread(packed, layer_count, layer)
+    packed, base = lax.optimization_barrier((packed, 2.0 * base))
     packed = lax.all_gather(packed, "core", axis=0, tiled=False)
     strips = packed[:, :, width:].sum(0).reshape(1, strip_count, lanes)
     small = spread(strips, section_count, "sections")
@@ -182,7 +183,6 @@
     p_hat = jnp.einsum("krd,krt->ktd", p_avg, gram_root[0], precision=highest)
     q_local = jnp.einsum("ktd,kdf->ktf", p_hat, combined, precision=highest)
     bundle = q_local.reshape(pairs * rank, lanes)
-    bundle, base = lax.optimization_barrier((bundle, base))
     q_set = lax.all_gather(bundle, shards, axis=0, tiled=False)
     q_set, small = lax.optimization_barrier((q_set, small))
 

time: 108 us -> 114 us (1.056)
  local copies, waits for them, and re-layouts: 1.87 us -> 4.74 us
  other arithmetic: 1.07 us -> 2.76 us
  blocking collectives: 51.8 us -> 53.2 us
    unnamed x13 -> x17, local copies, waits for them, and re-layouts: 0.07 us -> 2.94 us
    mul x0 -> x1, other arithmetic: none -> 1.67 us  [per_device(): packed, base = lax.optimization_barrier((packed, 2.0 * base))]
    all_gather x1, blocking collectives: 16.8 us -> 18.2 us  [per_device(): q_set = lax.all_gather(bundle, shards, axis=0, tiled=False)]
where the time goes in v6:
time: 114 us
  blocking collectives  53.2 us (47%)
  starting transfers between devices  16.6 us (15%)
  between operations  14.2 us (12%)
  waiting for transfers between devices  13.5 us (12%)
  Pallas kernels  5.18 us (5%)
  local copies, waits for them, and re-layouts  4.74 us (4%)
  matrix products  3.48 us (3%)
  other arithmetic  2.76 us (2%)
    all_to_all x1, blocking collectives, exchange(): return lax.all_to_all(blocks, axes, 0, 0, tiled=True)  24.6 us
    all_gather x1, blocking collectives, per_device(): q_set = lax.all_gather(bundle, shards, axis=0, tiled=False)  18.2 us
    all_to_all x3, starting transfers between devices, exchange(): return lax.all_to_all(blocks, axes, 0, 0, tiled=True)  16.6 us
    all_to_all x3, waiting for transfers between devices, exchange(): return lax.all_to_all(blocks, axes, 0, 0, tiled=True)  13.4 us
    all_gather x1, blocking collectives, per_device(): packed = lax.all_gather(packed, 'core', axis=0, tiled=False)  6.06 us
    all_gather x1, blocking collectives, per_device(): sent = lax.all_gather(sent, 'core', axis=0, tiled=False)  4.37 us
    pallas_call x1, Pallas kernels, per_device(): pl.pallas_call(finish_kernel, grid_spec=pltpu.PrefetchScalarGridSpec(num_...  3.24 us
    unnamed x17, local copies, waits for them, and re-layouts  2.94 us
  transfers between devices with their start and end apart: 4, of which 2 were waited for; matrix products, arithmetic and copies ran while one was open for 5% of the time, Pallas kernels for 0%

profile of v6, /device:TPU:1, one launch (start us, length us, event | category | flops | bytes accessed | tf_op | source)
XLA Modules:
  0.0 113.7 jit_solution(9050178804134506826)
XLA Ops:
  7.2 0.0 copy-start
  7.2 0.0 copy-start.1
  7.2 0.0 all-gather.4.cloned.1.call-start
  7.2 0.0 copy-start.2
  7.3 1.9 %prepare.1 = (f32[240,128]{1,0:T(8,128)}, f32[512,128]{1,0:T(8,128)}) custom-call(f32[192,128]{1,0:T(8,128)} %bitcast.73, f32[192,128]{1,0:T(8,128)} %bitcast.62, f32[40,96]{1,0:T(8,128)} %bitcast.74, f32[40,96]{1,0:T(8,128)} %bitcast.64, f32[2,96]{1,0:T(2,128)} %gain_weights.1, f32[2,96]{1,0:T(2,128)} %gain_momentum.3, bf16[40,1536]{1,0:T(8,128)(2,1)} %bitcast.72, ...), custom_call_target="tpu_custom_call" | custom-call | tf_op jit(solution)/shard_map/prepare/pallas_call | solution.py:142
  9.2 0.0 all-gather.4.cloned.1.call-update
  9.2 7.7 %all-to-all-start = ((f32[8,64,128]{2,1,0:T(8,128)}), f32[8,64,128]{2,1,0:T(8,128)S(1)}, u32[]{:S(2)}, u32[]{:S(2)}) async-start(f32[8,64,128]{2,1,0:T(8,128)} %bitcast.70), calls=%async_computation | async-start | bytes 524288 | tf_op jit(solution)/shard_map/all_to_all | solution.py:23
  16.9 0.8 reduce-precision_convert_fusion.1
  17.6 0.0 copy-done.1
  17.7 0.4 fusion.8
  18.0 0.0 copy-done.2
  18.0 0.4 convolution_add_fusion
  18.4 0.1 reduce_sum.36
  18.6 4.4 %all_gather.19 = f32[2,32,1536]{2,1,0:T(8,128)S(1)} all-gather(f32[1,32,1536]{2,1,0:T(8,128)S(1)} %constant_dynamic-slice_fusion), channel_id=1, replica_groups=mesh['stack'=8,'core'=2,'tensor'=4,'sections'=8] {'core'}, dimensions={0}, use_global_device_ids=true | all-gather | bytes 589824 | tf_op jit(solution)/shard_map/all_gather | solution.py:172
  23.0 3.3 %all-to-all-done = f32[8,64,128]{2,1,0:T(8,128)S(1)} async-done(((f32[8,64,128]{2,1,0:T(8,128)}), f32[8,64,128]{2,1,0:T(8,128)S(1)}, u32[]{:S(2)}, u32[]{:S(2)}) %all-to-all-start) | async-done | bytes 262176 | tf_op jit(solution)/shard_map/all_to_all | solution.py:23
  26.3 0.2 copy.20
  26.6 24.6 %all_to_all.28 = f32[32,1,1792]{2,1,0:T(1,128)S(1)} all-to-all(f32[32,1,1792]{2,1,0:T(1,128)S(1)} %copy.20), channel_id=1, replica_groups=mesh['stack'=8,'core'=2,'tensor'=4,'sections'=8] {'stack','tensor'}, dimensions={0} | all-to-all | bytes 458752 | tf_op jit(solution)/shard_map/all_to_all | solution.py:23
  51.2 0.1 reduce_sum.38
  51.3 0.8 broadcast_in_dim.26
  52.1 5.4 %all-to-all-start.2 = ((f32[32,1,1792]{2,1,0:T(1,128)}), f32[32,1,1792]{2,1,0:T(1,128)S(1)}, u32[]{:S(2)}, u32[]{:S(2)}) async-start(f32[32,1,1792]{2,1,0:T(1,128)} %broadcast_in_dim.26), calls=%async_computation.2 | async-start | bytes 458752 | tf_op jit(solution)/shard_map/all_to_all | solution.py:23
  57.5 10.1 %all-to-all-done.2 = f32[32,1,1792]{2,1,0:T(1,128)S(1)} async-done(((f32[32,1,1792]{2,1,0:T(1,128)}), f32[32,1,1792]{2,1,0:T(1,128)S(1)}, u32[]{:S(2)}, u32[]{:S(2)}) %all-to-all-start.2) | async-done | bytes 229408 | tf_op jit(solution)/shard_map/all_to_all | solution.py:23
  67.7 0.0 all-gather.4.cloned.1.call-done
  67.7 1.7 %broadcast_multiply_fusion = f32[3840,128]{1,0:T(8,128)S(1)} fusion(f32[3840,128]{1,0:T(8,128)} %all-gather.4.cloned.1.call-done), kind=kLoop, calls=%fused_computation.5 | loop fusion | flops 491520 | bytes 3932160 | tf_op jit(solution)/shard_map/mul | solution.py:177
  69.4 6.1 %all-gather.1 = f32[64,1792]{1,0:T(8,128)S(1)} all-gather(f32[32,1792]{1,0:T(8,128)S(1)} %bitcast.69), channel_id=3, replica_groups=mesh['stack'=8,'core'=2,'tensor'=4,'sections'=8] {'core'}, dimensions={0}, use_global_device_ids=true | all-gather | bytes 688128 | tf_op jit(solution)/shard_map/all_gather | solution.py:178
  75.5 0.0 copy-done
  75.5 0.5 fusion.4
  76.0 0.7 broadcast_in_dim.28
  76.7 0.0 copy-start.5
  76.7 0.0 copy-start.7
  76.7 3.5 %all-to-all-start.3 = ((f32[8,64,128]{2,1,0:T(8,128)}), f32[8,64,128]{2,1,0:T(8,128)S(1)}, u32[]{:S(2)}, u32[]{:S(2)}) async-start(f32[8,64,128]{2,1,0:T(8,128)} %broadcast_in_dim.28), calls=%async_computation.3 | async-start | bytes 524288 | tf_op jit(solution)/shard_map/all_to_all | solution.py:23
  80.3 2.2 %fusion = f32[2,32,128]{2,1,0:T(8,128)S(1)} fusion(f32[2,1536,32]{1,2,0:T(8,128)S(1)} %fusion.4, bf16[1,1,2,1536,128]{4,3,2,1,0:T(8,128)(2,1)} %param.13, bf16[1,1,2,1536,128]{4,3,2,1,0:T(8,128)(2,1)S(1)} %copy-done.1), kind=kOutput, calls=%fused_computation.1 | convolution fusion | flops 152174592 | bytes 1998848 | tf_op jit(solution)/shard_map/ktd,kdf->ktf/dot_general | solution.py:184
  82.5 18.2 %all_gather.24.q_set = f32[16,64,128]{2,1,0:T(8,128)} all-gather(f32[1,64,128]{2,1,0:T(8,128)S(1)} %bitcast.71), channel_id=1, replica_groups=mesh['stack'=8,'core'=2,'tensor'=4,'sections'=8] {'stack','core'}, dimensions={0}, use_global_device_ids=true | all-gather | bytes 557056 | tf_op jit(solution)/shard_map/all_gather | solution.py:186
  100.7 0.0 all-to-all-done.3
  100.7 0.0 copy-done.5
  100.7 0.0 copy-done.7
  100.7 0.0 copy-start.3
  100.7 1.1 copy-done.3
  101.8 0.0 copy-start.4
  101.8 1.0 copy-done.4
  102.8 0.0 copy-start.6
  102.8 0.7 copy-done.6
  103.6 3.2 %finish.1 = (bf16[2,1536,128]{2,1,0:T(8,128)(2,1)}, f32[2,96,128]{2,1,0:T(8,128)}, f32[2,1536,128]{2,1,0:T(8,128)}, f32[40,96]{1,0:T(8,128)}, f32[40,1536]{1,0:T...) custom-call(s32[1]{0:T(128)} %bitcast.index, f32[16,64,128]{2,1,0:T(8,128)S(1)} %copy-done.4, f32[2,32,1536]{2,1,0:T(8,128)S(1)} %bitcast.60, ...), custom_call_target="tpu_custom_call" | custom-call | tf_op jit(solution)/shard_map/finish/pallas_call | solution.py:195
  (8 shorter events, 0.1 us)
Async XLA Ops:
  7.2 68.3 %copy-start = (f32[1,2,32,32]{3,2,1,0:T(8,128)S(1)}, f32[1,2,32,32]{3,2,1,0:T(8,128)}, u32[]{:S(2)}) copy-start(f32[1,2,32,32]{3,2,1,0:T(8,128)} %param.15) | copy-start | bytes 24580
  7.2 10.5 %copy-start.1 = (bf16[1,1,2,1536,128]{4,3,2,1,0:T(8,128)(2,1)S(1)}, bf16[1,1,2,1536,128]{4,3,2,1,0:T(8,128)(2,1)}, u32[]{:S(2)}) copy-start(bf16[1,1,2,1536,128]{4,3,2,1,0:T(8,128)(2,1)} %param.12) | copy-start | bytes 2359300
  7.2 60.5 %all-gather.4.cloned.1.call-start = ((), (), s32[]{:S(2)}) async-start(), calls=%async_computation.4 | async-start | bytes 2088960 | tf_op jit(solution)/shard_map/all_gather | solution.py:159
  7.2 10.8 %copy-start.2 = (bf16[1,1,2,1536,128]{4,3,2,1,0:T(8,128)(2,1)S(1)}, bf16[1,1,2,1536,128]{4,3,2,1,0:T(8,128)(2,1)}, u32[]{:S(2)}) copy-start(bf16[1,1,2,1536,128]{4,3,2,1,0:T(8,128)(2,1)} %param.13) | copy-start | bytes 2359300
  9.2 17.1 %all-to-all-start = ((f32[8,64,128]{2,1,0:T(8,128)}), f32[8,64,128]{2,1,0:T(8,128)S(1)}, u32[]{:S(2)}, u32[]{:S(2)}) async-start(f32[8,64,128]{2,1,0:T(8,128)} %bitcast.70), calls=%async_computation | async-start | bytes 524288 | tf_op jit(solution)/shard_map/all_to_all | solution.py:23
  52.1 15.5 %all-to-all-start.2 = ((f32[32,1,1792]{2,1,0:T(1,128)}), f32[32,1,1792]{2,1,0:T(1,128)S(1)}, u32[]{:S(2)}, u32[]{:S(2)}) async-start(f32[32,1,1792]{2,1,0:T(1,128)} %broadcast_in_dim.26), calls=%async_computation.2 | async-start | bytes 458752 | tf_op jit(solution)/shard_map/all_to_all | solution.py:23
  76.7 24.0 %copy-start.5 = (f32[1,2,96,128]{3,2,1,0:T(8,128)S(1)}, f32[1,2,96,128]{3,2,1,0:T(8,128)}, u32[]{:S(2)}) copy-start(f32[1,2,96,128]{3,2,1,0:T(8,128)} %param.16) | copy-start | bytes 294916
  76.7 24.0 %copy-start.7 = (f32[2,96]{1,0:T(2,128)S(1)}, f32[2,96]{1,0:T(2,128)}, u32[]{:S(2)}) copy-start(f32[2,96]{1,0:T(2,128)} %gain_momentum.3) | copy-start | bytes 2308
  76.7 23.9 %all-to-all-start.3 = ((f32[8,64,128]{2,1,0:T(8,128)}), f32[8,64,128]{2,1,0:T(8,128)S(1)}, u32[]{:S(2)}, u32[]{:S(2)}) async-start(f32[8,64,128]{2,1,0:T(8,128)} %broadcast_in_dim.28), calls=%async_computation.3 | async-start | bytes 524288 | tf_op jit(solution)/shard_map/all_to_all | solution.py:23
  100.7 1.1 copy-start.3
  101.8 1.0 copy-start.4
  102.8 0.7 copy-start.6
Sparse Core Ops, SparseCore 0:
  10.7 49.3 all-gather.3
